TPU v7x, 32 devices: a whole 2x2x4 slice. The times are simulated.
32 devices in a mesh: rows: 8 (over z, x), cols: 4 (over y, core).
Axes of the slice: x: 2, y: 2, z: 4, core: 2. Of those that a mesh axis runs over, the one named last changes fastest.
Arguments:
- cell_bin: int32 [1048576], P(('rows', 'cols')), may hold values from 0 to 32767
- cell_area: bfloat16 [1048576], P(('rows', 'cols')), may hold values from 0.5 to 4
- owner: int32 [1048576], P(('rows', 'cols')), may hold values from 0 to 31, as said below
- net_box: int32 [4, 524288], P(None, ('rows', 'cols')), may hold values from 0 to 511, as said below
Outputs:
- density: float32 [512, 2048], P('rows', 'cols')
- migrated: float32 [3, 2097152], P(None, ('rows', 'cols'))
- migrated_bin: int32 [2097152], P(('rows', 'cols'))
Inputs may be any that keep to these rules, and one draw needn't show every extreme that they name: No tile names one owner for more than 2048 of its cells, and some owner is named exactly 2048 times by every tile. `net_box`: each column holds a box inside the net's tile with first row <= last row < 64 and first column <= last column.
All inputs are finite; a program needn't handle non-finite values.
Results may differ from a plain program's by a relative error of at most 0.0003.
Values sent between devices are 32-bit elements; how exact they have to be, the bound alone decides.
No kernel may reach another device: no remote copies, remote signals or barrier semaphores. Data moves between devices by JAX's collectives and lax.ppermute only.
A program may use at most 192 MiB of HBM per device.

v0:
```python
import jax
import jax.numpy as jnp
from jax import lax
from jax.sharding import PartitionSpec as P

TILE_R = 64
TILE_C = 512
DIFF_STEPS = 4


RATE = 0.2
GAMMA = 0.05


def with_halo(shard, sides, width):
    for axis, dim in sides:
        size, length = (lax.axis_size(axis), shard.shape[dim])
        up = [(i, (i + 1) % size) for i in range(size - 1)]
        down = [(j, i) for i, j in up]
        last = lax.slice_in_dim(shard, length - width, length, axis=dim)
        leading = lax.slice_in_dim(shard, 0, width, axis=dim)
        before = lax.ppermute(last, axis, up)
        after = lax.ppermute(leading, axis, down)
        shard = jnp.concatenate([before, shard, after], axis=dim)
    return shard


def splat_cells(cell_bin, cell_area):
    count = cell_bin.shape[0]
    block_size = min(8192, count)
    rows_of = (cell_bin // TILE_C).reshape(-1, block_size)
    cols_of = (cell_bin % TILE_C).reshape(-1, block_size)
    areas = cell_area.reshape(-1, block_size)
    row_iota = lax.broadcasted_iota(jnp.int32, (TILE_R, block_size), 0)
    col_iota = lax.broadcasted_iota(jnp.int32, (block_size, TILE_C), 1)

    def splat_add_block(running, inputs):
        rows_here, cols_here, area_here = inputs
        picker = (row_iota == rows_here[None, :]).astype(jnp.bfloat16)
        placed = jnp.where(
            col_iota == cols_here[:, None], area_here[:, None], jnp.zeros((), jnp.bfloat16)
        )
        return (running + jnp.dot(picker, placed, preferred_element_type=jnp.float32), None)

    running, unused = lax.scan(
        splat_add_block, jnp.zeros((TILE_R, TILE_C), jnp.float32), (rows_of, cols_of, areas)
    )
    return running


def congestion_map(net_box):
    count = net_box.shape[1]
    block_size = min(8192, count)
    boxes = net_box.reshape(4, -1, block_size).transpose(1, 0, 2)
    row_iota = lax.broadcasted_iota(jnp.int32, (TILE_R, block_size), 0)
    col_iota = lax.broadcasted_iota(jnp.int32, (block_size, TILE_C), 1)

    def congestion_add_block(running, box):
        tall = (box[1] - box[0] + 1).astype(jnp.float32)
        wide = (box[3] - box[2] + 1).astype(jnp.float32)
        weight = ((tall + wide) / (tall * wide)).astype(jnp.bfloat16)
        cover_rows = ((row_iota >= box[0][None, :]) & (row_iota <= box[1][None, :])).astype(
            jnp.bfloat16
        )
        cover_cols = (col_iota >= box[2][:, None]) & (col_iota <= box[3][:, None])
        weighted = jnp.where(cover_cols, weight[:, None], jnp.zeros((), jnp.bfloat16))
        return (running + jnp.dot(cover_rows, weighted, preferred_element_type=jnp.float32), None)

    running, unused = lax.scan(
        congestion_add_block, jnp.zeros((TILE_R, TILE_C), jnp.float32), boxes
    )
    return running


def advance(padded, row_base, col_base, grid_rows, grid_cols):
    rows_inner = padded.shape[0] - 2
    cols_inner = padded.shape[1] - 2
    center = padded[1:-1, 1:-1]
    global_rows = row_base + 1 + lax.broadcasted_iota(jnp.int32, (rows_inner, 1), 0)
    global_cols = col_base + 1 + lax.broadcasted_iota(jnp.int32, (1, cols_inner), 1)
    inside_rows = (global_rows >= 0) & (global_rows < grid_rows)
    inside_cols = (global_cols >= 0) & (global_cols < grid_cols)
    open_lower = (inside_rows & (global_rows + 1 < grid_rows)).astype(jnp.float32)
    open_upper = (inside_rows & (global_rows >= 1)).astype(jnp.float32)
    open_right = (inside_cols & (global_cols + 1 < grid_cols)).astype(jnp.float32)
    open_left = (inside_cols & (global_cols >= 1)).astype(jnp.float32)
    lower = (padded[2:, 1:-1] - center) * open_lower
    upper = (padded[:-2, 1:-1] - center) * open_upper
    right = (padded[1:-1, 2:] - center) * open_right
    left = (padded[1:-1, :-2] - center) * open_left
    spread = 2.0 * (center + 1.0)
    after = center + RATE * (lower + upper + (right + left))
    return (after, -(lower - upper) / spread, -(right - left) / spread)


def owner_slots(owner, devices, capacity):
    count = owner.shape[0]
    block_size = min(8192, count)
    owner_blocks = owner.reshape(-1, block_size)
    dest_iota = lax.broadcasted_iota(jnp.int32, (block_size, devices), 1)

    def rank_block(seen, owner_here):
        hits = (owner_here[:, None] == dest_iota).astype(jnp.int32)
        before = jnp.cumsum(hits, axis=0) - hits
        ranks = jnp.sum((before + seen[None, :]) * hits, axis=1)
        return (seen + jnp.sum(hits, axis=0), ranks)

    unused, ranks = lax.scan(rank_block, jnp.zeros((devices,), jnp.int32), owner_blocks)
    return owner * capacity + ranks.reshape(-1)


def pack_slots(records, fills, slots, devices, capacity):
    width = records.shape[1]
    buffer = jnp.broadcast_to(fills[None, :], (devices * capacity, width))
    buffer = buffer.at[slots].set(records)
    return buffer.T.reshape(width, devices, capacity)


def on_device(cell_bin, cell_area, owner, net_box):
    devices = lax.axis_size(("rows", "cols"))
    count = cell_bin.shape[0]
    capacity = 2 * count // devices
    slots = owner_slots(owner, devices, capacity)
    area = cell_area.astype(jnp.float32)
    bin_float = cell_bin.astype(jnp.float32)
    raw = splat_cells(cell_bin, cell_area)
    congestion = congestion_map(net_box)
    dens = raw * (1.0 + GAMMA * congestion)
    grid_rows = lax.axis_size("rows") * TILE_R
    grid_cols = lax.axis_size("cols") * TILE_C
    row_start = lax.axis_index("rows") * TILE_R
    col_start = lax.axis_index("cols") * TILE_C
    flow_row = jnp.zeros((TILE_R, TILE_C), jnp.float32)
    flow_col = jnp.zeros((TILE_R, TILE_C), jnp.float32)
    for step in range(DIFF_STEPS):
        padded = with_halo(dens, (("rows", 0), ("cols", 1)), 1)
        dens, speed_row, speed_col = advance(
            padded, row_start - 1, col_start - 1, grid_rows, grid_cols
        )
        flow_row = flow_row + speed_row
        flow_col = flow_col + speed_col
    flow_table = jnp.stack([flow_row.reshape(-1), flow_col.reshape(-1)], axis=1)
    shifts = flow_table[cell_bin]
    records = jnp.concatenate([shifts, area[:, None], bin_float[:, None]], axis=1)
    whole_pack = pack_slots(
        records, jnp.array([0.0, 0.0, 0.0, -1.0], jnp.float32), slots, devices, capacity
    )
    received = lax.all_to_all(whole_pack, ("rows", "cols"), split_axis=1, concat_axis=1, tiled=True)
    migrated = received[:3].reshape(3, -1)
    migrated_bin = received[3].reshape(-1).astype(jnp.int32)
    return (dens, migrated, migrated_bin)


def solution(mesh):
    in_specs = (
        P(("rows", "cols")),
        P(("rows", "cols")),
        P(("rows", "cols")),
        P(None, ("rows", "cols")),
    )
    out_specs = (P("rows", "cols"), P(None, ("rows", "cols")), P(("rows", "cols")))
    return jax.shard_map(
        on_device, mesh=mesh, in_specs=in_specs, out_specs=out_specs, check_vma=False
    )
```

profile of v0, /device:TPU:0, one launch (start us, length us, event | category | flops | bytes accessed | tf_op | source)
XLA Modules:
  0.0 467.2 jit_solution(3291815804677557236)
XLA Ops:
  0.6 0.9 reshape.144
  1.5 9.9 %while.38 = (s32[]{:T(128)}, f32[64,512]{1,0:T(8,128)S(1)}, s32[2,4,8192]{2,1,0:T(4,128)}, s32[]{:T(128)}, s32[]{:T(128)}, /*index=5*/s32[]{}, s32[]{}, s32[]{}) while((s32[]{:T(128)}, f32[64,512]{1,0:T(8,128)S(1)}, s32[2,4,8192]{2,1,0:T(4,128)}, s32[]{:T(128)}, s32[]{:T(128)}, /*index=5*/s32[]{}, s32[]{}, s32[]{}) %tuple.98), condition=%wide.region_3.4_spmd.clone.clone, body=%wide.region_2.3_spmd.clone.clone.sunk | while | flops 555368448 | bytes 819355 | solution.py:69
  1.5 1.3 constant_dynamic-slice_fusion.12
  2.9 3.6 fusion.107
  6.5 1.3 constant_dynamic-slice_fusion.12
  7.8 3.6 fusion.107
  11.7 11.7 %while.36 = (s32[]{:T(128)}, f32[64,512]{1,0:T(8,128)S(1)}, s32[4,8192]{1,0:T(4,128)S(1)}, s32[4,8192]{1,0:T(4,128)S(1)}, bf16[4,8192]{1,0:T(4,128)(2,1)S(1)}, /*index=5*/s32[]{:T(128)}, s32[]{:T(128)}) while((s32[]{:T(128)}, f32[64,512]{1,0:T(8,128)S(1)}, s32[4,8192]{1,0:T(4,128)S(1)}, s32[4,8192]{1,0:T(4,128)S(1)}, ...), condition=%wide.region_1.0_spmd.clone, body=%wide.region_0.1_spmd.clone.sunk | while | flops 545849344 | bytes 508007 | solution.py:45
  11.9 2.7 fusion.102
  14.9 2.7 fusion.102
  17.8 2.7 fusion.102
  20.7 2.7 fusion.102
  23.5 4.9 %collective-permute-start.1 = (f32[1,512]{1,0:T(1,128)S(1)}, f32[1,512]{1,0:T(1,128)S(1)}, u32[]{:S(2)}, u32[]{:S(2)}) collective-permute-start(f32[1,512]{1,0:T(1,128)S(1)} %get-tuple-element.225), channel_id=1, source_target_pairs={{0,4},{4,8},{8,12},{12,16},{16,20},{20,24},{24,28},{1,5},{5,9},{9,... | collective-permute-start | bytes 6152 | tf_op jit(solution)/shard_map/ppermute | solution.py:22
  28.4 1.3 collective-permute-start
  29.7 4.1 collective-permute-done
  33.9 1.3 collective-permute-start.2
  35.2 3.0 collective-permute-start.3
  38.3 0.8 collective-permute-done.3
  39.3 4.4 collective-permute-start.5
  43.7 1.3 collective-permute-start.4
  45.0 4.2 collective-permute-done.4
  49.2 1.3 collective-permute-start.6
  50.5 3.0 collective-permute-start.7
  53.6 0.8 collective-permute-done.7
  54.6 3.4 collective-permute-start.9
  58.0 1.3 collective-permute-start.8
  59.5 4.1 collective-permute-done.8
  63.6 1.3 collective-permute-start.10
  64.9 4.5 collective-permute-start.11
  69.4 62.3 %while.37 = (s32[]{:T(128)}, s32[32]{0:T(128)}, s32[4,8192]{1,0:T(4,128)S(1)}, s32[4,8192]{1,0:T(4,128)S(1)}, s32[]{:T(128)}, /*index=5*/s32[]{:T(128)}) while((s32[]{:T(128)}, s32[32]{0:T(128)}, s32[4,8192]{1,0:T(4,128)S(1)}, s32[4,8192]{1,0:T(4,128)S(1)}, s32[]{:T(128)}, /*index=5*/s32[]{:T(128)}) %tuple.93), condition=%wide.region_9.10_spmd.clone, body=%wide.region_4.0_spmd.clone.sunk | while | flops 36036640 | bytes 8660072 | solution.py:108
  70.3 9.5 %reduce-window.14 = s32[32,64,128]{2,1,0:T(8,128)S(1)} reduce-window(s32[32,64,128]{2,1,0:T(8,128)S(1)} %bitcast.76, s32[]{:T(128)} %constant.63.clone.1..sunk.1), window={size=1x1x128 pad=0_0x0_0x127_0}, to_apply=%region_6.6 | reduce-window | flops 33292288 | bytes 2097156 | tf_op jit(solution)/shard_map/reduce-window
  79.8 0.9 slice_reduce_fusion.2
  81.3 1.6 fusion.103
  84.0 1.2 broadcast_select_fusion.2
  85.5 9.5 %reduce-window.14 = s32[32,64,128]{2,1,0:T(8,128)S(1)} reduce-window(s32[32,64,128]{2,1,0:T(8,128)S(1)} %bitcast.76, s32[]{:T(128)} %constant.63.clone.1..sunk.1), window={size=1x1x128 pad=0_0x0_0x127_0}, to_apply=%region_6.6 | reduce-window | flops 33292288 | bytes 2097156 | tf_op jit(solution)/shard_map/reduce-window
  95.1 0.9 slice_reduce_fusion.2
  96.6 1.6 fusion.103
  98.2 1.2 fusion.104
  99.9 1.2 broadcast_select_fusion.2
  101.5 9.5 %reduce-window.14 = s32[32,64,128]{2,1,0:T(8,128)S(1)} reduce-window(s32[32,64,128]{2,1,0:T(8,128)S(1)} %bitcast.76, s32[]{:T(128)} %constant.63.clone.1..sunk.1), window={size=1x1x128 pad=0_0x0_0x127_0}, to_apply=%region_6.6 | reduce-window | flops 33292288 | bytes 2097156 | tf_op jit(solution)/shard_map/reduce-window
  111.0 0.9 slice_reduce_fusion.2
  112.5 1.6 fusion.103
  114.1 1.2 fusion.104
  115.8 1.2 broadcast_select_fusion.2
  117.4 9.5 %reduce-window.14 = s32[32,64,128]{2,1,0:T(8,128)S(1)} reduce-window(s32[32,64,128]{2,1,0:T(8,128)S(1)} %bitcast.76, s32[]{:T(128)} %constant.63.clone.1..sunk.1), window={size=1x1x128 pad=0_0x0_0x127_0}, to_apply=%region_6.6 | reduce-window | flops 33292288 | bytes 2097156 | tf_op jit(solution)/shard_map/reduce-window
  126.9 0.9 slice_reduce_fusion.2
  128.4 1.6 fusion.103
  130.0 1.2 fusion.104
  131.8 1.0 multiply_add_fusion.1
  132.8 4.4 collective-permute-start.13
  137.1 1.5 collective-permute-start.12
  138.8 8.1 %copy.23 = f32[32768,1]{1,0:T(8,128)} copy(f32[32768,1]{0,1:T(1,128)S(1)} %bitcast.94) | data formatting | bytes 262144 | tf_op jit(solution)/shard_map/broadcast_in_dim | solution.py:144
  146.9 8.1 %copy.24 = f32[32768,1]{1,0:T(8,128)} copy(f32[32768,1]{0,1:T(1,128)S(1)} %bitcast.93) | data formatting | bytes 262144 | tf_op jit(solution)/shard_map/broadcast_in_dim | solution.py:144
  155.0 1.3 collective-permute-start.14
  156.3 6.0 %collective-permute-start.15 = (f32[66,1]{1,0:T(8,128)S(1)}, f32[66,1]{1,0:T(8,128)S(1)}, u32[]{:S(2)}, u32[]{:S(2)}) collective-permute-start(f32[66,1]{1,0:T(8,128)S(1)} %get-tuple-element.208), channel_id=1, source_target_pairs={{0,1},{1,2},{2,3},{4,5},{5,6},{6,7},{8,9},{9,10},{10,11},{12,13},{... | collective-permute-start | bytes 800 | tf_op jit(solution)/shard_map/ppermute | solution.py:22
  164.1 8.3 %copy.22 = f32[32768,2]{1,0:T(8,128)} copy(f32[32768,2]{0,1:T(2,128)S(1)} %pad_maximum_fusion) | data formatting | bytes 524288 | tf_op jit(solution)/shard_map/stack | solution.py:142
  172.4 114.1 %gather_fusion = f32[32768,2]{1,0:T(8,128)} fusion(f32[32768,2]{1,0:T(8,128)} %copy.22, s32[32768]{0:T(1024)S(1)} %get-tuple-element.215), kind=kCustom, calls=%fused_computation | custom fusion | bytes 655360 | tf_op jit(solution)/shard_map/gather | solution.py:143
  286.4 11.0 %broadcast_in_dim.59 = f32[65536,4]{1,0:T(8,128)} broadcast(f32[4]{0:T(128)S(1)} %copy-done.15), dimensions={1} | broadcast | bytes 1048592 | tf_op jit(solution)/shard_map/broadcast_in_dim | solution.py:114
  297.5 115.8 %scatter_custom_fusion = f32[65536,4]{1,0:T(8,128)} fusion(f32[65536,4]{1,0:T(8,128)} %broadcast_in_dim.59, s32[32768]{0:T(1024)S(1)} %compare_select_fusion, f32[32768,1]{1,0:T(8,128)} %copy.24, f32[]{:T(128)} %constant.110, f32[32768,1]{1,0:T(8,128)} %copy.23, f32[32768,2]{1,0:T(8,128)} %gather_fusion), kind=kCustom, calls=%fused_computation.51 | custom fusion | flops 262144 | bytes 51380736 | tf_op jit(solution)/shard_map/scatter | solution.py:115
  413.3 18.4 %copy.25 = f32[4,32,2048]{2,0,1:T(4,128)} copy(f32[4,32,2048]{0,2,1:T(8,128)} %bitcast.74) | data formatting | bytes 2097152 | tf_op jit(solution)/shard_map/reshape | solution.py:116
  431.7 7.3 %all-to-all-start = ((f32[4,32,2048]{2,0,1:T(4,128)}), f32[4,32,2048]{2,0,1:T(4,128)S(1)}, u32[]{:S(2)}, u32[]{:S(2)}) async-start(f32[4,32,2048]{2,0,1:T(4,128)} %copy.25), calls=%async_computation | async-start | bytes 2097152 | tf_op jit(solution)/shard_map/all_to_all | solution.py:148
  439.0 0.8 multiply_add_fusion
  439.9 25.4 %all-to-all-done = f32[4,32,2048]{2,0,1:T(4,128)S(1)} async-done(((f32[4,32,2048]{2,0,1:T(4,128)}), f32[4,32,2048]{2,0,1:T(4,128)S(1)}, u32[]{:S(2)}, u32[]{:S(2)}) %all-to-all-start) | async-done | bytes 1048608 | tf_op jit(solution)/shard_map/all_to_all | solution.py:148
  465.2 1.0 slice_convert_fusion
  466.2 1.0 copy.60
  (108 shorter events, 9.9 us)
Async XLA Ops:
  1.5 9.9 %copy-start.2 = (s32[32768]{0:T(1024)S(1)}, s32[32768]{0:T(1024)}, u32[]{:S(2)}) copy-start(s32[32768]{0:T(1024)} %param.11) | copy-start | bytes 393220
  11.7 47.7 %copy-start = (s32[32768]{0:T(1024)S(1)}, s32[32768]{0:T(1024)}, u32[]{:S(2)}) copy-start(s32[32768]{0:T(1024)} %param.13) | copy-start | bytes 393220
  23.5 6.2 %collective-permute-start.1 = (f32[1,512]{1,0:T(1,128)S(1)}, f32[1,512]{1,0:T(1,128)S(1)}, u32[]{:S(2)}, u32[]{:S(2)}) collective-permute-start(f32[1,512]{1,0:T(1,128)S(1)} %get-tuple-element.225), channel_id=1, source_target_pairs={{0,4},{4,8},{8,12},{12,16},{16,20},{20,24},{24,28},{1,5},{5,9},{9,... | collective-permute-start | bytes 6152 | tf_op jit(solution)/shard_map/ppermute | solution.py:22
  28.4 5.5 %collective-permute-start = (f32[1,512]{1,0:T(1,128)S(1)}, f32[1,512]{1,0:T(1,128)S(1)}, u32[]{:S(2)}, u32[]{:S(2)}) collective-permute-start(f32[1,512]{1,0:T(1,128)S(1)} %get-tuple-element.226), channel_id=1, source_target_pairs={{4,0},{8,4},{12,8},{16,12},{20,16},{24,20},{28,24},{5,1},{9,5},{13... | collective-permute-start | bytes 6152 | tf_op jit(solution)/shard_map/ppermute | solution.py:23
  33.9 4.4 collective-permute-start.2
  35.2 3.9 collective-permute-start.3
  38.3 16.3 %copy-start.11 = (f32[64]{0:T(128)}, f32[64]{0:T(128)S(1)}, u32[]{:S(2)}) copy-start(f32[64]{0:T(128)S(1)} %get-tuple-element.229) | copy-start | bytes 772
  38.3 19.7 %copy-start.13 = (f32[64]{0:T(128)}, f32[64]{0:T(128)S(1)}, u32[]{:S(2)}) copy-start(f32[64]{0:T(128)S(1)} %get-tuple-element.230) | copy-start | bytes 772
  39.3 5.7 %collective-permute-start.5 = (f32[1,512]{1,0:T(1,128)S(1)}, f32[1,512]{1,0:T(1,128)S(1)}, u32[]{:S(2)}, u32[]{:S(2)}) collective-permute-start(f32[1,512]{1,0:T(1,128)S(1)} %get-tuple-element.223), channel_id=1, source_target_pairs={{0,4},{4,8},{8,12},{12,16},{16,20},{20,24},{24,28},{1,5},{5,9},{9,... | collective-permute-start | bytes 6152 | tf_op jit(solution)/shard_map/ppermute | solution.py:22
  43.7 5.5 %collective-permute-start.4 = (f32[1,512]{1,0:T(1,128)S(1)}, f32[1,512]{1,0:T(1,128)S(1)}, u32[]{:S(2)}, u32[]{:S(2)}) collective-permute-start(f32[1,512]{1,0:T(1,128)S(1)} %get-tuple-element.224), channel_id=1, source_target_pairs={{4,0},{8,4},{12,8},{16,12},{20,16},{24,20},{28,24},{5,1},{9,5},{13... | collective-permute-start | bytes 6152 | tf_op jit(solution)/shard_map/ppermute | solution.py:23
  45.0 24.4 %copy-start.3 = (f32[1,512]{1,0:T(1,128)}, f32[1,512]{1,0:T(1,128)S(1)}, u32[]{:S(2)}) copy-start(f32[1,512]{1,0:T(1,128)S(1)} %collective-permute-done.5) | copy-start | bytes 6148
  49.2 20.2 %copy-start.5 = (f32[1,512]{1,0:T(1,128)}, f32[1,512]{1,0:T(1,128)S(1)}, u32[]{:S(2)}) copy-start(f32[1,512]{1,0:T(1,128)S(1)} %collective-permute-done.4) | copy-start | bytes 6148
  49.2 4.3 collective-permute-start.6
  50.5 3.9 collective-permute-start.7
  54.6 4.8 %collective-permute-start.9 = (f32[1,512]{1,0:T(1,128)S(1)}, f32[1,512]{1,0:T(1,128)S(1)}, u32[]{:S(2)}, u32[]{:S(2)}) collective-permute-start(f32[1,512]{1,0:T(1,128)S(1)} %get-tuple-element.221), channel_id=1, source_target_pairs={{0,4},{4,8},{8,12},{12,16},{16,20},{20,24},{24,28},{1,5},{5,9},{9,... | collective-permute-start | bytes 6152 | tf_op jit(solution)/shard_map/ppermute | solution.py:22
  58.0 5.5 %collective-permute-start.8 = (f32[1,512]{1,0:T(1,128)S(1)}, f32[1,512]{1,0:T(1,128)S(1)}, u32[]{:S(2)}, u32[]{:S(2)}) collective-permute-start(f32[1,512]{1,0:T(1,128)S(1)} %get-tuple-element.222), channel_id=1, source_target_pairs={{4,0},{8,4},{12,8},{16,12},{20,16},{24,20},{28,24},{5,1},{9,5},{13... | collective-permute-start | bytes 6152 | tf_op jit(solution)/shard_map/ppermute | solution.py:23
  59.4 10.0 %copy-start.7 = (f32[1,512]{1,0:T(1,128)}, f32[1,512]{1,0:T(1,128)S(1)}, u32[]{:S(2)}) copy-start(f32[1,512]{1,0:T(1,128)S(1)} %collective-permute-done.9) | copy-start | bytes 6148
  63.5 5.9 %copy-start.9 = (f32[1,512]{1,0:T(1,128)}, f32[1,512]{1,0:T(1,128)S(1)}, u32[]{:S(2)}) copy-start(f32[1,512]{1,0:T(1,128)S(1)} %collective-permute-done.8) | copy-start | bytes 6148
  63.6 68.2 %collective-permute-start.10 = (f32[66,1]{1,0:T(8,128)S(1)}, f32[66,1]{1,0:T(8,128)S(1)}, u32[]{:S(2)}, u32[]{:S(2)}) collective-permute-start(f32[66,1]{1,0:T(8,128)S(1)} %get-tuple-element.209), channel_id=1, source_target_pairs={{1,0},{2,1},{3,2},{5,4},{6,5},{7,6},{9,8},{10,9},{11,10},{13,12},{... | collective-permute-start | bytes 800 | tf_op jit(solution)/shard_map/ppermute | solution.py:23
  64.9 66.9 %collective-permute-start.11 = (f32[66,1]{1,0:T(8,128)S(1)}, f32[66,1]{1,0:T(8,128)S(1)}, u32[]{:S(2)}, u32[]{:S(2)}) collective-permute-start(f32[66,1]{1,0:T(8,128)S(1)} %get-tuple-element.210), channel_id=1, source_target_pairs={{0,1},{1,2},{2,3},{4,5},{5,6},{6,7},{8,9},{9,10},{10,11},{12,13},{... | collective-permute-start | bytes 800 | tf_op jit(solution)/shard_map/ppermute | solution.py:22
  69.4 69.2 %copy-start.1 = (bf16[32768]{0:T(1024)(128)(2,1)S(1)}, bf16[32768]{0:T(1024)(128)(2,1)}, u32[]{:S(2)}) copy-start(bf16[32768]{0:T(1024)(128)(2,1)} %param.12) | copy-start | bytes 196612
  132.8 22.2 %collective-permute-start.13 = (f32[1,512]{1,0:T(1,128)S(1)}, f32[1,512]{1,0:T(1,128)S(1)}, u32[]{:S(2)}, u32[]{:S(2)}) collective-permute-start(f32[1,512]{1,0:T(1,128)S(1)} %get-tuple-element.219), channel_id=1, source_target_pairs={{0,4},{4,8},{8,12},{12,16},{16,20},{20,24},{24,28},{1,5},{5,9},{9,... | collective-permute-start | bytes 6152 | tf_op jit(solution)/shard_map/ppermute | solution.py:22
  137.1 17.8 %collective-permute-start.12 = (f32[1,512]{1,0:T(1,128)S(1)}, f32[1,512]{1,0:T(1,128)S(1)}, u32[]{:S(2)}, u32[]{:S(2)}) collective-permute-start(f32[1,512]{1,0:T(1,128)S(1)} %get-tuple-element.220), channel_id=1, source_target_pairs={{4,0},{8,4},{12,8},{16,12},{20,16},{24,20},{28,24},{5,1},{9,5},{13... | collective-permute-start | bytes 6152 | tf_op jit(solution)/shard_map/ppermute | solution.py:23
  138.7 23.7 %copy-start.4 = (f32[1,512]{1,0:T(1,128)S(1)}, f32[1,512]{1,0:T(1,128)}, u32[]{:S(2)}) copy-start(f32[1,512]{1,0:T(1,128)} %copy-done.3) | copy-start | bytes 6148
  138.7 23.7 %copy-start.6 = (f32[1,512]{1,0:T(1,128)S(1)}, f32[1,512]{1,0:T(1,128)}, u32[]{:S(2)}) copy-start(f32[1,512]{1,0:T(1,128)} %copy-done.5) | copy-start | bytes 6148
  138.7 23.7 %copy-start.8 = (f32[1,512]{1,0:T(1,128)S(1)}, f32[1,512]{1,0:T(1,128)}, u32[]{:S(2)}) copy-start(f32[1,512]{1,0:T(1,128)} %copy-done.7) | copy-start | bytes 6148
  138.7 23.7 %copy-start.10 = (f32[1,512]{1,0:T(1,128)S(1)}, f32[1,512]{1,0:T(1,128)}, u32[]{:S(2)}) copy-start(f32[1,512]{1,0:T(1,128)} %copy-done.9) | copy-start | bytes 6148
  138.7 23.7 %copy-start.12 = (f32[64]{0:T(128)S(1)}, f32[64]{0:T(128)}, u32[]{:S(2)}) copy-start(f32[64]{0:T(128)} %copy-done.11) | copy-start | bytes 772
  138.7 23.7 %copy-start.14 = (f32[64]{0:T(128)S(1)}, f32[64]{0:T(128)}, u32[]{:S(2)}) copy-start(f32[64]{0:T(128)} %copy-done.13) | copy-start | bytes 772
  155.0 7.8 %collective-permute-start.14 = (f32[66,1]{1,0:T(8,128)S(1)}, f32[66,1]{1,0:T(8,128)S(1)}, u32[]{:S(2)}, u32[]{:S(2)}) collective-permute-start(f32[66,1]{1,0:T(8,128)S(1)} %get-tuple-element.207), channel_id=1, source_target_pairs={{1,0},{2,1},{3,2},{5,4},{6,5},{7,6},{9,8},{10,9},{11,10},{13,12},{... | collective-permute-start | bytes 800 | tf_op jit(solution)/shard_map/ppermute | solution.py:23
  156.3 6.9 %collective-permute-start.15 = (f32[66,1]{1,0:T(8,128)S(1)}, f32[66,1]{1,0:T(8,128)S(1)}, u32[]{:S(2)}, u32[]{:S(2)}) collective-permute-start(f32[66,1]{1,0:T(8,128)S(1)} %get-tuple-element.208), channel_id=1, source_target_pairs={{0,1},{1,2},{2,3},{4,5},{5,6},{6,7},{8,9},{9,10},{10,11},{12,13},{... | collective-permute-start | bytes 800 | tf_op jit(solution)/shard_map/ppermute | solution.py:22
  172.4 114.1 %copy-start.15 = (f32[4]{0:T(128)S(1)}, f32[4]{0:T(128)}, u32[]{:S(2)}) copy-start(f32[4]{0:T(128)} %constant.107.clone) | copy-start | bytes 52
  431.7 33.6 %all-to-all-start = ((f32[4,32,2048]{2,0,1:T(4,128)}), f32[4,32,2048]{2,0,1:T(4,128)S(1)}, u32[]{:S(2)}, u32[]{:S(2)}) async-start(f32[4,32,2048]{2,0,1:T(4,128)} %copy.25), calls=%async_computation | async-start | bytes 2097152 | tf_op jit(solution)/shard_map/all_to_all | solution.py:148
where the time goes:
time: 468 us; the launch traced here: 467 us
  local copies, waits for them, and re-layouts  180 us (38%)
  other arithmetic  176 us (38%)
  starting transfers between devices  51.4 us (11%)
  waiting for transfers between devices  39.7 us (8%)
  matrix products  18.1 us (4%)
    scatter x1, other arithmetic, pack_slots(): buffer = buffer.at[slots].set(records)  116 us
    gather x1, local copies, waits for them, and re-layouts, on_device(): shifts = flow_table[cell_bin]  114 us
    another operation x12, other arithmetic  40.3 us
    ppermute x8, starting transfers between devices, with_halo(): before = lax.ppermute(last, axis, up)  33.5 us
    all_to_all x1, waiting for transfers between devices, on_device(): lax.all_to_all(whole_pack, ('rows', 'cols'), split_axis=1, concat_axis=1,...  25.4 us
    reshape x1, local copies, waits for them, and re-layouts, pack_slots(): return buffer.T.reshape(width, devices, capacity)  18.4 us
    ppermute x8, waiting for transfers between devices, with_halo(): after = lax.ppermute(leading, axis, down)  12.4 us
    broadcast_in_dim x1, local copies, waits for them, and re-layouts, pack_slots(): buffer = jnp.broadcast_to(fills[None, :], (devices * capacity, width))  11 us
  transfers between devices with their start and end apart: 17, of which 7 were waited for; matrix products, arithmetic and copies ran while one was open for 17% of the time, Pallas kernels for 0%

commit v1 on v0

v1 whole, which is shorter than its diff:
```python
import functools
import jax
import jax.numpy as jnp
from jax import lax
from jax.experimental import pallas as pl
from jax.experimental.pallas import tpu as pltpu
from jax.sharding import PartitionSpec as P

TILE_R = 64
TILE_C = 512
DIFF_STEPS = 4
RATE = 0.2
GAMMA = 0.05
LANES = 128
EDGE = 8
GROUP = 16
BF16 = jnp.bfloat16
F32 = jnp.float32


def dot_nt(a, b):
    return lax.dot_general(a, b, (((1,), (1,)), ((), ())), preferred_element_type=F32)


def sublane_iota(rows, lanes=LANES):
    return lax.broadcasted_iota(jnp.int32, (rows, lanes), 0)


def narrow(x):
    return x.astype(F32).astype(BF16)


def spread(row, rows):
    lanes = row.shape[1]
    packed = jnp.broadcast_to(row, (16, lanes)).astype(BF16)
    return jnp.broadcast_to(packed[None], (rows // 16, 16, lanes)).reshape(rows, lanes)


def density_kernel(bin_ref, area_ref, box_ref, dens_ref, top_ref, bottom_ref, s_ref, w_ref, a_ref, raw_ref, cong_ref):
    bins = bin_ref[...]
    s_ref[...] = (((bins >> 8) & 1) * TILE_R + (bins >> 9)).astype(F32)
    w_ref[...] = (bins & 255).astype(F32)
    a_ref[...] = area_ref[...].astype(F32)
    raw_ref[...] = jnp.zeros_like(raw_ref)
    cong_ref[...] = jnp.zeros_like(cong_ref)
    nil = jnp.zeros((), BF16)
    one = jnp.ones((), BF16)
    s_iota = narrow(sublane_iota(2 * TILE_R))
    w_iota = narrow(sublane_iota(256))

    def cells(step, carry):
        left, right = [], []
        for k in range(GROUP):
            r = step * GROUP + k
            here = pl.ds(r, 1)
            hit = s_iota == spread(s_ref[here, :], 2 * TILE_R)
            left.append(jnp.where(hit, spread(a_ref[here, :], 2 * TILE_R), nil))
            right.append(jnp.where(w_iota == spread(w_ref[here, :], 256), one, nil))
        raw_ref[...] += dot_nt(jnp.concatenate(left, axis=1), jnp.concatenate(right, axis=1))
        return carry

    lax.fori_loop(0, bin_ref.shape[0] // GROUP, cells, 0)
    width = GROUP * LANES
    r_iota = narrow(sublane_iota(TILE_R, width))
    c_iota = narrow(sublane_iota(TILE_C, width) - TILE_C // 2)

    def nets(step, carry):
        box = box_ref[:, pl.ds(pl.multiple_of(step * width, width), width)].astype(F32)
        tall = box[1:2] - box[0:1] + 1.0
        wide = box[3:4] - box[2:3] + 1.0
        weight = (tall + wide) / (tall * wide)
        rows = (r_iota >= spread(box[0:1], TILE_R)) & (r_iota <= spread(box[1:2], TILE_R))
        half = float(TILE_C // 2)
        cols = (c_iota >= spread(box[2:3] - half, TILE_C)) & (c_iota <= spread(box[3:4] - half, TILE_C))
        cong_ref[...] += dot_nt(
            jnp.where(rows, one, nil), jnp.where(cols, spread(weight, TILE_C), nil)
        )
        return carry

    lax.fori_loop(0, box_ref.shape[1] // width, nets, 0)
    raw = jnp.concatenate([raw_ref[:TILE_R], raw_ref[TILE_R:]], axis=1)
    dens = raw * (1.0 + GAMMA * cong_ref[...])
    dens_ref[...] = dens
    top_ref[...] = dens[:EDGE]
    bottom_ref[...] = dens[TILE_R - EDGE :]


def expand(parts, starts_ref, total, pairs):
    per = pairs[0][2].shape[-2]
    lane = lax.broadcasted_iota(jnp.int32, (per, LANES), 1)
    place = sublane_iota(per) * LANES + lane

    def one_owner(o, carry):
        start = starts_ref[0, o]
        stop = jnp.where(o + 1 < parts, starts_ref[0, jnp.minimum(o + 1, parts - 1)], total)
        row = start // LANES
        shift = start - row * LANES
        back = lax.rem(LANES - shift, LANES)
        keep = place < stop - start
        near = lane < LANES - shift
        for source, slot, target, fill in pairs:
            a = pltpu.roll(source[pl.ds(row, per), :], back, 1)
            b = pltpu.roll(source[pl.ds(row + 1, per), :], back, 1)
            target[o, slot] = jnp.where(keep, jnp.where(near, a, b), fill)
        return carry

    lax.fori_loop(0, parts, one_owner, 0)


def order_kernel(parts, owner_ref, bin_ref, area_ref, slots_ref, sorted_ref, starts_ref,
                 pre_ref, cnt_ref, s_ref, w_ref, bh_ref, bl_ref, ar_ref, acc_ref, b_ref, a_ref, vec_ref, smem_ref, sem):
    rows = owner_ref.shape[0]
    i = sublane_iota(LANES, 2 * LANES)
    j = lax.broadcasted_iota(jnp.int32, (LANES, 2 * LANES), 1)
    upper = narrow(i < j)
    block = 64
    lane = lax.broadcasted_iota(jnp.int32, (block, LANES), 1)
    many = 8

    def rank_rows(c, carry):
        here = pl.ds(pl.multiple_of(c * block, block), block)
        owner = owner_ref[here, :]

        def step(g, both):
            prefix, counts = both
            hits = [owner == g * many + k for k in range(many)]
            sums = jnp.dot(jnp.concatenate([narrow(h) for h in hits], axis=0), upper, preferred_element_type=F32)
            for k in range(many):
                part = sums[k * block : (k + 1) * block]
                prefix = jnp.where(hits[k], part[:, :LANES], prefix)
                counts = jnp.where(lane == g * many + k, part[:, LANES:], counts)
            return prefix, counts

        zero = jnp.zeros((block, LANES), F32)
        prefix, counts = lax.fori_loop(0, parts // many, step, (zero, zero))
        pre_ref[here, :] = prefix
        cnt_ref[here, :] = counts
        return carry

    lax.fori_loop(0, rows // block, rank_rows, 0)
    counts = cnt_ref[...]
    lower = narrow(lax.broadcasted_iota(jnp.int32, (rows, rows), 1) < lax.broadcasted_iota(jnp.int32, (rows, rows), 0))
    base = jnp.dot(lower, counts.astype(BF16), preferred_element_type=F32)
    total = base[rows - 8 :] + counts[rows - 8 :]
    high = jnp.floor(total * (1.0 / 64.0))
    low = total - high * 64.0
    strict = upper[:, :LANES]
    first = jnp.dot(low.astype(BF16), strict, preferred_element_type=F32) + 64.0 * jnp.dot(
        high.astype(BF16), strict, preferred_element_type=F32
    )
    starts = jnp.broadcast_to(first[7:8], (8, LANES))
    vec_ref[...] = starts.astype(jnp.int32)
    starts_ref[...] = starts.astype(jnp.int32)
    copy = pltpu.make_async_copy(vec_ref, smem_ref, sem)
    copy.start()
    dest = (pre_ref[...] + jnp.take_along_axis(base + starts[:1], owner_ref[...], axis=1)).astype(jnp.int32)
    half = rows // 2
    top = jnp.where(dest >= half * LANES, 1, 0)
    s_ref[...] = ((dest >> 7) - top * half).astype(F32)
    w_ref[...] = ((dest & (LANES - 1)) + top * LANES).astype(F32)
    bins = bin_ref[...]
    bh_ref[...] = (bins >> 8).astype(F32)
    bl_ref[...] = (bins & 255).astype(F32)
    ar_ref[...] = area_ref[...].astype(F32)
    acc_ref[...] = jnp.zeros_like(acc_ref)
    nil = jnp.zeros((), BF16)
    one = jnp.ones((), BF16)
    s_iota = narrow(sublane_iota(half))
    w_iota = narrow(sublane_iota(2 * LANES))

    def place(step, carry):
        left, right = [], []
        for k in range(GROUP):
            here = pl.ds(step * GROUP + k, 1)
            hit = s_iota == spread(s_ref[here, :], half)
            left.append(
                jnp.concatenate(
                    [jnp.where(hit, spread(x[here, :], half), nil) for x in (bh_ref, bl_ref, ar_ref)], axis=0
                )
            )
            right.append(jnp.where(w_iota == spread(w_ref[here, :], 2 * LANES), one, nil))
        acc_ref[...] += dot_nt(jnp.concatenate(left, axis=1), jnp.concatenate(right, axis=1))
        return carry

    lax.fori_loop(0, rows // GROUP, place, 0)
    for h in range(2):
        cols = slice(h * LANES, (h + 1) * LANES)
        out = slice(h * half, (h + 1) * half)
        b_ref[out, :] = acc_ref[:half, cols] * 256.0 + acc_ref[half : 2 * half, cols]
        a_ref[out, :] = acc_ref[2 * half :, cols]
    pad = slice(rows, b_ref.shape[0])
    b_ref[pad, :] = jnp.zeros((b_ref.shape[0] - rows, LANES), F32)
    a_ref[pad, :] = jnp.zeros((b_ref.shape[0] - rows, LANES), F32)
    sorted_ref[...] = b_ref[:rows]
    copy.wait()
    expand(parts, smem_ref, rows * LANES, ((b_ref, 0, slots_ref, -1.0), (a_ref, 1, slots_ref, 0.0)))


def flow_kernel(parts, grid_rows, grid_cols, starts_ref, place_ref, dens_in, up_ref, down_ref, left_ref, right_ref, sorted_ref,
                dens_ref, slots_ref, pad_ref, hi_ref, lo_ref, row_ref, col_ref):
    rows = sorted_ref.shape[0]
    mid = pl.ds(EDGE, TILE_R)
    inner = pl.ds(LANES, TILE_C)
    pad_ref[mid, inner] = dens_in[...]
    pad_ref[:EDGE, inner] = up_ref[...]
    pad_ref[TILE_R + EDGE :, inner] = down_ref[...]
    pad_ref[:, :LANES] = left_ref[...]
    pad_ref[:, LANES + TILE_C :] = right_ref[...]
    tall, wide = pad_ref.shape
    grow = place_ref[0] + lax.broadcasted_iota(jnp.int32, (tall, 1), 0) - EDGE
    gcol = place_ref[1] + lax.broadcasted_iota(jnp.int32, (1, wide), 1) - LANES
    open_lower = grow + 1 != grid_rows
    open_upper = grow != 0
    open_right = gcol + 1 != grid_cols
    open_left = gcol != 0
    flow_row = jnp.zeros((TILE_R, TILE_C), F32)
    flow_col = jnp.zeros((TILE_R, TILE_C), F32)
    for step in range(DIFF_STEPS):
        d = pad_ref[...]
        lower = jnp.where(open_lower, pltpu.roll(d, tall - 1, 0) - d, 0.0)
        upper = jnp.where(open_upper, pltpu.roll(d, 1, 0) - d, 0.0)
        right = jnp.where(open_right, pltpu.roll(d, wide - 1, 1) - d, 0.0)
        left = jnp.where(open_left, pltpu.roll(d, 1, 1) - d, 0.0)
        pad_ref[...] = d + RATE * ((lower + upper) + (right + left))
        centre = (slice(EDGE, EDGE + TILE_R), slice(LANES, LANES + TILE_C))
        rate = -0.5 / (d[centre] + 1.0)
        flow_row += (lower - upper)[centre] * rate
        flow_col += (right - left)[centre] * rate
    dens_ref[...] = pad_ref[mid, inner]
    coarse, fine = [], []
    for flow in (flow_row, flow_col):
        table = jnp.concatenate([flow[:, k * LANES : (k + 1) * LANES] for k in range(TILE_C // LANES)], axis=0).T
        big = table.astype(BF16)
        coarse.append(big)
        fine.append((table - big.astype(F32)).astype(BF16))
    table = jnp.concatenate(coarse + fine, axis=0)
    bins = sorted_ref[...].astype(jnp.int32)
    hi_ref[...] = (((bins >> 7) & 3) * TILE_R + (bins >> 9)).astype(F32)
    lo_ref[...] = (bins & (LANES - 1)).astype(F32)
    hi_iota = narrow(sublane_iota(256))
    lo_iota = sublane_iota(LANES).astype(F32)
    nil = jnp.zeros((), BF16)
    one = jnp.ones((), BF16)
    group = 8

    def look_up(step, carry):
        picks = jnp.concatenate(
            [
                jnp.where(hi_iota == spread(hi_ref[pl.ds(step * group + k, 1), :], 256), one, nil)
                for k in range(group)
            ],
            axis=1,
        )
        found = jnp.dot(table, picks, preferred_element_type=F32)
        for k in range(group):
            here = pl.ds(step * group + k, 1)
            hit = lo_iota == lo_ref[here, :]
            part = found[:, k * LANES : (k + 1) * LANES]
            both = part[: 2 * LANES] + part[2 * LANES :]
            row_ref[here, :] = jnp.sum(jnp.where(hit, both[:LANES], 0.0), axis=0, keepdims=True)
            col_ref[here, :] = jnp.sum(jnp.where(hit, both[LANES:], 0.0), axis=0, keepdims=True)
        return carry

    lax.fori_loop(0, rows // group, look_up, 0)
    pad = slice(rows, row_ref.shape[0])
    row_ref[pad, :] = jnp.zeros((row_ref.shape[0] - rows, LANES), F32)
    col_ref[pad, :] = jnp.zeros((row_ref.shape[0] - rows, LANES), F32)
    expand(parts, starts_ref, rows * LANES, ((row_ref, 0, slots_ref, 0.0), (col_ref, 1, slots_ref, 0.0)))


def shape(*dims, dtype=F32):
    return jax.ShapeDtypeStruct(dims, dtype)


def vmem(*dims, dtype=F32):
    return pltpu.VMEM(dims, dtype)


def on_device(cell_bin, cell_area, owner, net_box):
    parts = lax.axis_size(("rows", "cols"))
    count = cell_bin.shape[0]
    rows = count // LANES
    capacity = 2 * count // parts
    per = capacity // LANES
    spare = -(-(per + 1) // 8) * 8
    bins = cell_bin.reshape(rows, LANES)
    area = cell_area.reshape(rows, LANES)
    n_rows, n_cols = lax.axis_size("rows"), lax.axis_size("cols")
    grid_rows, grid_cols = n_rows * TILE_R, n_cols * TILE_C
    dens, top, bottom = pl.pallas_call(
        density_kernel,
        out_shape=(shape(TILE_R, TILE_C), shape(EDGE, TILE_C), shape(EDGE, TILE_C)),
        scratch_shapes=[vmem(rows, LANES)] * 3 + [vmem(2 * TILE_R, 256), vmem(TILE_R, TILE_C)],
        name="density",
    )(bins, area, net_box)
    ahead = [(k, k + 1) for k in range(n_rows - 1)]
    behind = [(k + 1, k) for k in range(n_rows - 1)]
    up = lax.ppermute(bottom, "rows", ahead)
    down = lax.ppermute(top, "rows", behind)
    slots, in_order, starts = pl.pallas_call(
        functools.partial(order_kernel, parts),
        out_shape=(shape(parts, 2, per, LANES), shape(rows, LANES), shape(8, LANES, dtype=jnp.int32)),
        scratch_shapes=[vmem(rows, LANES)] * 7
        + [vmem(3 * rows // 2, 2 * LANES), vmem(rows + spare, LANES), vmem(rows + spare, LANES),
           vmem(8, LANES, dtype=jnp.int32), pltpu.SMEM((8, LANES), jnp.int32), pltpu.SemaphoreType.DMA],
        cost_estimate=pl.CostEstimate(flops=15_000_000_000, bytes_accessed=2_000_000, transcendentals=0),
        name="order",
    )(owner.reshape(rows, LANES), bins, area)
    strip = jnp.concatenate([up, dens, down], axis=0)
    ahead = [(k, k + 1) for k in range(n_cols - 1)]
    behind = [(k + 1, k) for k in range(n_cols - 1)]
    left = lax.ppermute(strip[:, TILE_C - LANES :], "cols", ahead)
    right = lax.ppermute(strip[:, :LANES], "cols", behind)
    first = lax.all_to_all(slots, ("rows", "cols"), 0, 0, tiled=True)
    place = jnp.stack([lax.axis_index("rows") * TILE_R, lax.axis_index("cols") * TILE_C]).astype(jnp.int32)
    whole = pl.BlockSpec(memory_space=pltpu.VMEM)
    scalars = pl.BlockSpec(memory_space=pltpu.SMEM)
    density, shifts = pl.pallas_call(
        functools.partial(flow_kernel, parts, grid_rows, grid_cols),
        out_shape=(shape(TILE_R, TILE_C), shape(parts, 2, per, LANES)),
        in_specs=[scalars, scalars] + [whole] * 6,
        scratch_shapes=[vmem(TILE_R + 2 * EDGE, TILE_C + 2 * LANES), vmem(rows, LANES), vmem(rows, LANES),
                        vmem(rows + spare, LANES), vmem(rows + spare, LANES)],
        cost_estimate=pl.CostEstimate(flops=15_000_000_000, bytes_accessed=2_000_000, transcendentals=0),
        name="flow",
    )(starts, place, dens, up, down, left, right, in_order)
    second = lax.all_to_all(shifts, ("rows", "cols"), 0, 0, tiled=True)
    migrated = jnp.stack([second[:, 0].reshape(-1), second[:, 1].reshape(-1), first[:, 1].reshape(-1)])
    return density, migrated, first[:, 0].reshape(-1).astype(jnp.int32)


def solution(mesh):
    both = ("rows", "cols")
    in_specs = (P(both), P(both), P(both), P(None, both))
    out_specs = (P("rows", "cols"), P(None, both), P(both))
    return jax.shard_map(on_device, mesh=mesh, in_specs=in_specs, out_specs=out_specs, check_vma=False)
```

time: 468 us -> 100 us (0.21)
  local copies, waits for them, and re-layouts: 180 us -> 1.81 us
  other arithmetic: 176 us -> 2.95 us
  Pallas kernels: 0 us -> 53.5 us
  starting transfers between devices: 51.4 us -> 25.7 us
  waiting for transfers between devices: 39.7 us -> 15.2 us
  matrix products: 18.1 us -> 0 us
    scatter x1 -> x0, other arithmetic: 116 us -> none  [pack_slots(): buffer = buffer.at[slots].set(records)]
    gather x1 -> x0, local copies, waits for them, and re-layouts: 114 us -> none  [on_device(): shifts = flow_table[cell_bin]]
    pallas_call x0 -> x3, Pallas kernels: none -> 53.5 us  [the longest x1 19.8 us: on_device(): pl.pallas_call(functools.partial(flow_kernel, parts, grid_rows, grid_cols...]
    another operation x13 -> x2, other arithmetic: 40.6 us -> 2.21 us  [the longest x1 1.65 us: on_device(): jnp.stack([second[:, 0].reshape(-1), second[:, 1].reshape(-1), first[:, 1...]
    ppermute x16 -> x4, starting transfers between devices: 44 us -> 10.5 us  [the longest x1 4.86 us: on_device(): up = lax.ppermute(bottom, 'rows', ahead)]
    broadcast_in_dim x3 -> x0, local copies, waits for them, and re-layouts: 27.2 us -> none  [the longest x1 11 us: pack_slots(): buffer = jnp.broadcast_to(fills[None, :], (devices * capacity, width))]
    reshape x5 -> x0, local copies, waits for them, and re-layouts: 19.4 us -> none  [the longest x1 18.4 us: pack_slots(): return buffer.T.reshape(width, devices, capacity)]
    dot_general x6 -> x0, matrix products: 18.1 us -> none  [the longest x4 10.9 us: splat_add_block(): jnp.dot(picker, placed, preferred_element_type=jnp.float32)]
  transfers between devices with their start and end apart: 17 -> 6, of which waited for: 7 -> 2; matrix products, arithmetic and copies ran while one was open for 17% -> 1% of each run, Pallas kernels for 0% -> 38%
where the time goes in v1:
time: 100 us; the launch traced here: 99.9 us
  Pallas kernels  53.5 us (54%)
  starting transfers between devices  25.7 us (26%)
  waiting for transfers between devices  15.2 us (15%)
  other arithmetic  2.95 us (3%)
  local copies, waits for them, and re-layouts  1.81 us (2%)
    pallas_call x1, Pallas kernels, on_device(): pl.pallas_call(functools.partial(flow_kernel, parts, grid_rows, grid_cols...  19.8 us
    pallas_call x1, Pallas kernels, on_device(): pl.pallas_call(functools.partial(order_kernel, parts), out_shape=(shape(p...  18 us
    pallas_call x1, Pallas kernels, on_device(): pl.pallas_call(density_kernel, out_shape=(shape(TILE_R, TILE_C), shape(ED...  15.6 us
    all_to_all x1, waiting for transfers between devices, on_device(): second = lax.all_to_all(shifts, ('rows', 'cols'), 0, 0, tiled=True)  14.9 us
    all_to_all x1, starting transfers between devices, on_device(): second = lax.all_to_all(shifts, ('rows', 'cols'), 0, 0, tiled=True)  8.16 us
    all_to_all x1, starting transfers between devices, on_device(): first = lax.all_to_all(slots, ('rows', 'cols'), 0, 0, tiled=True)  7.04 us
    ppermute x1, starting transfers between devices, on_device(): up = lax.ppermute(bottom, 'rows', ahead)  4.86 us
    ppermute x1, starting transfers between devices, on_device(): left = lax.ppermute(strip[:, TILE_C - LANES:], 'cols', ahead)  3.03 us
  transfers between devices with their start and end apart: 6, of which 2 were waited for; matrix products, arithmetic and copies ran while one was open for 1% of the time, Pallas kernels for 38%

profile of v1, /device:TPU:0, one launch (start us, length us, event | category | flops | bytes accessed | tf_op | source)
XLA Modules:
  0.0 99.9 jit_solution(7723694771166807645)
XLA Ops:
  0.6 15.6 %density.1 = (f32[64,512]{1,0:T(8,128)}, f32[8,512]{1,0:T(8,128)}, f32[8,512]{1,0:T(8,128)}) custom-call(s32[256,128]{1,0:T(8,128)} %bitcast.13, bf16[256,128]{1,0:T(8,128)(2,1)} %bitcast.15, s32[4,16384]{1,0:T(4,128)} %box_ref.1), custom_call_target="tpu_custom_call" | custom-call | tf_op jit(solution)/shard_map/density/pallas_call | solution.py:290
  16.3 4.9 %collective-permute-start = (f32[8,512]{1,0:T(8,128)}, f32[8,512]{1,0:T(8,128)S(1)}, u32[]{:S(2)}, u32[]{:S(2)}) collective-permute-start(f32[8,512]{1,0:T(8,128)} %get-tuple-element.13), channel_id=1, source_target_pairs={{0,4},{4,8},{8,12},{12,16},{16,20},{20,24},{24,28},{1,5},{5,9},{9,... | collective-permute-start | bytes 49160 | tf_op jit(solution)/shard_map/ppermute | solution.py:298
  21.1 1.3 %collective-permute-start.1 = (f32[8,512]{1,0:T(8,128)}, f32[8,512]{1,0:T(8,128)S(1)}, u32[]{:S(2)}, u32[]{:S(2)}) collective-permute-start(f32[8,512]{1,0:T(8,128)} %get-tuple-element.14), channel_id=1, source_target_pairs={{4,0},{8,4},{12,8},{16,12},{20,16},{24,20},{28,24},{5,1},{9,5},{13... | collective-permute-start | bytes 49160 | tf_op jit(solution)/shard_map/ppermute | solution.py:299
  22.4 18.0 %order.1 = (f32[32,2,16,128]{3,2,1,0:T(8,128)}, f32[256,128]{1,0:T(8,128)}, s32[8,128]{1,0:T(8,128)}) custom-call(s32[256,128]{1,0:T(8,128)} %bitcast.17, s32[256,128]{1,0:T(8,128)} %bitcast.14, bf16[256,128]{1,0:T(8,128)(2,1)} %bitcast.16), custom_call_target="tpu_custom_call" | custom-call | flops 15000000512 | bytes 2000000 | tf_op jit(solution)/shard_map/order/pallas_call | solution.py:300
  40.5 0.0 copy-start
  40.5 7.0 %all-to-all-start.1 = ((f32[32,2,16,128]{3,2,1,0:T(8,128)}), f32[32,2,16,128]{3,2,1,0:T(8,128)S(1)}, u32[]{:S(2)}, u32[]{:S(2)}) async-start(f32[32,2,16,128]{3,2,1,0:T(8,128)} %get-tuple-element.18), calls=%async_computation.1 | async-start | bytes 1048576 | tf_op jit(solution)/shard_map/all_to_all | solution.py:314
  47.5 0.0 collective-permute-done.up_ref
  47.6 0.0 copy-start.1
  47.6 0.6 copy-done.1
  48.2 0.0 copy-done
  48.2 0.0 collective-permute-done.1.down_ref
  48.2 0.0 copy-start.2
  48.2 0.6 copy-done.2
  48.8 1.3 %collective-permute-start.3 = (f32[80,128]{1,0:T(8,128)S(1)}, f32[80,128]{1,0:T(8,128)S(1)}, u32[]{:S(2)}, u32[]{:S(2)}) collective-permute-start(f32[80,128]{1,0:T(8,128)S(1)} %get-tuple-element.23), channel_id=1, source_target_pairs={{1,0},{2,1},{3,2},{5,4},{6,5},{7,6},{9,8},{10,9},{11,10},{13,12},{... | collective-permute-start | bytes 122888 | tf_op jit(solution)/shard_map/ppermute | solution.py:313
  50.1 3.0 %collective-permute-start.2 = (f32[80,128]{1,0:T(8,128)S(1)}, f32[80,128]{1,0:T(8,128)S(1)}, u32[]{:S(2)}, u32[]{:S(2)}) collective-permute-start(f32[80,128]{1,0:T(8,128)S(1)} %get-tuple-element.24), channel_id=1, source_target_pairs={{0,1},{1,2},{2,3},{4,5},{5,6},{6,7},{8,9},{9,10},{10,11},{12,13},{... | collective-permute-start | bytes 122888 | tf_op jit(solution)/shard_map/ppermute | solution.py:312
  53.1 0.6 pad_add_fusion.place_ref
  53.7 0.0 collective-permute-done.3.right_ref
  53.7 0.0 copy-start.3
  53.7 0.3 collective-permute-done.2.left_ref
  54.0 0.0 copy-start.4
  54.0 0.3 copy-done.3
  54.3 0.3 copy-done.4
  54.6 19.8 %flow.1 = (f32[64,512]{1,0:T(8,128)}, f32[32,2,16,128]{3,2,1,0:T(8,128)}) custom-call(s32[8,128]{1,0:T(8,128)} %get-tuple-element.11.starts_ref, s32[2]{0:T(128)} %pad_add_fusion.place_ref, f32[64,512]{1,0:T(8,128)} %get-tuple-element.12.dens_in, f32[8,512]{1,0:T(8,128)} %copy-done.1, f32[8,512]{1,0:T(8,128)} %copy-done.2, f32[80,128]{1,0:T(8,128)} %copy-done.4, ...), custom_call_target="tpu_custom_call" | custom-call | flops 15000000512 | bytes 2000000 | tf_op jit(solution)/shard_map/flow/pallas_call | solution.py:318
  74.4 0.0 all-to-all-done.1
  74.4 8.2 %all-to-all-start = ((f32[32,2,16,128]{3,2,1,0:T(8,128)}), f32[32,2,16,128]{3,2,1,0:T(8,128)S(1)}, u32[]{:S(2)}, u32[]{:S(2)}) async-start(f32[32,2,16,128]{3,2,1,0:T(8,128)} %get-tuple-element.17), calls=%async_computation | async-start | bytes 1048576 | tf_op jit(solution)/shard_map/all_to_all | solution.py:327
  82.6 0.7 slice_convert_fusion
  83.3 14.9 %all-to-all-done = f32[32,2,16,128]{3,2,1,0:T(8,128)S(1)} async-done(((f32[32,2,16,128]{3,2,1,0:T(8,128)}), f32[32,2,16,128]{3,2,1,0:T(8,128)S(1)}, u32[]{:S(2)}, u32[]{:S(2)}) %all-to-all-start) | async-done | bytes 524320 | tf_op jit(solution)/shard_map/all_to_all | solution.py:327
  98.2 1.6 %pad_maximum_fusion = f32[3,65536]{1,0:T(4,128)} fusion(f32[1,65536]{1,0:T(1,128)S(1)} %bitcast.9, f32[1,65536]{1,0:T(1,128)S(1)} %bitcast.11, f32[1,65536]{1,0:T(1,128)S(1)} %bitcast.10), kind=kLoop, calls=%fused_computation | loop fusion | flops 393216 | bytes 1572864 | tf_op jit(solution)/shard_map/stack | solution.py:328
  (5 shorter events, 0.1 us)
Async XLA Ops:
  16.3 31.3 %collective-permute-start = (f32[8,512]{1,0:T(8,128)}, f32[8,512]{1,0:T(8,128)S(1)}, u32[]{:S(2)}, u32[]{:S(2)}) collective-permute-start(f32[8,512]{1,0:T(8,128)} %get-tuple-element.13), channel_id=1, source_target_pairs={{0,4},{4,8},{8,12},{12,16},{16,20},{20,24},{24,28},{1,5},{5,9},{9,... | collective-permute-start | bytes 49160 | tf_op jit(solution)/shard_map/ppermute | solution.py:298
  21.1 27.0 %collective-permute-start.1 = (f32[8,512]{1,0:T(8,128)}, f32[8,512]{1,0:T(8,128)S(1)}, u32[]{:S(2)}, u32[]{:S(2)}) collective-permute-start(f32[8,512]{1,0:T(8,128)} %get-tuple-element.14), channel_id=1, source_target_pairs={{4,0},{8,4},{12,8},{16,12},{20,16},{24,20},{28,24},{5,1},{9,5},{13... | collective-permute-start | bytes 49160 | tf_op jit(solution)/shard_map/ppermute | solution.py:299
  40.5 7.7 %copy-start = (f32[64,512]{1,0:T(8,128)S(1)}, f32[64,512]{1,0:T(8,128)}, u32[]{:S(2)}) copy-start(f32[64,512]{1,0:T(8,128)} %get-tuple-element.12.dens_in) | copy-start | bytes 393220
  40.5 33.9 %all-to-all-start.1 = ((f32[32,2,16,128]{3,2,1,0:T(8,128)}), f32[32,2,16,128]{3,2,1,0:T(8,128)S(1)}, u32[]{:S(2)}, u32[]{:S(2)}) async-start(f32[32,2,16,128]{3,2,1,0:T(8,128)} %get-tuple-element.18), calls=%async_computation.1 | async-start | bytes 1048576 | tf_op jit(solution)/shard_map/all_to_all | solution.py:314
  47.6 0.6 copy-start.1
  48.2 0.6 copy-start.2
  48.8 4.9 %collective-permute-start.3 = (f32[80,128]{1,0:T(8,128)S(1)}, f32[80,128]{1,0:T(8,128)S(1)}, u32[]{:S(2)}, u32[]{:S(2)}) collective-permute-start(f32[80,128]{1,0:T(8,128)S(1)} %get-tuple-element.23), channel_id=1, source_target_pairs={{1,0},{2,1},{3,2},{5,4},{6,5},{7,6},{9,8},{10,9},{11,10},{13,12},{... | collective-permute-start | bytes 122888 | tf_op jit(solution)/shard_map/ppermute | solution.py:313
  50.1 3.9 %collective-permute-start.2 = (f32[80,128]{1,0:T(8,128)S(1)}, f32[80,128]{1,0:T(8,128)S(1)}, u32[]{:S(2)}, u32[]{:S(2)}) collective-permute-start(f32[80,128]{1,0:T(8,128)S(1)} %get-tuple-element.24), channel_id=1, source_target_pairs={{0,1},{1,2},{2,3},{4,5},{5,6},{6,7},{8,9},{9,10},{10,11},{12,13},{... | collective-permute-start | bytes 122888 | tf_op jit(solution)/shard_map/ppermute | solution.py:312
  53.7 0.6 copy-start.3
  54.0 0.6 copy-start.4
  74.4 23.8 %all-to-all-start = ((f32[32,2,16,128]{3,2,1,0:T(8,128)}), f32[32,2,16,128]{3,2,1,0:T(8,128)S(1)}, u32[]{:S(2)}, u32[]{:S(2)}) async-start(f32[32,2,16,128]{3,2,1,0:T(8,128)} %get-tuple-element.17), calls=%async_computation | async-start | bytes 1048576 | tf_op jit(solution)/shard_map/all_to_all | solution.py:327

commit v2 on v1

--- a/solution.py
+++ b/solution.py
@@ -13,8 +13,13 @@
 GAMMA = 0.05
 LANES = 128
 EDGE = 8
-GROUP = 16
+GROUP = 32
+DIRECT = 8
+BY_DOT = 12
 BF16 = jnp.bfloat16
+F8 = jnp.float8_e4m3fn
+SMALL = 64.0
+MIDDLE = 16384
 F32 = jnp.float32
 
 
@@ -36,50 +41,62 @@
     return jnp.broadcast_to(packed[None], (rows // 16, 16, lanes)).reshape(rows, lanes)
 
 
-def density_kernel(bin_ref, area_ref, box_ref, dens_ref, top_ref, bottom_ref, s_ref, w_ref, a_ref, raw_ref, cong_ref):
+def halves(x):
+    big = x.astype(F8).astype(F32)
+    return big, x - big
+
+
+def density_kernel(bin_ref, area_ref, box_ref, dens_ref, top_ref, bottom_ref, s_ref, w_ref, a_ref, b_ref, raw_ref, cong_ref):
     bins = bin_ref[...]
     s_ref[...] = (((bins >> 8) & 1) * TILE_R + (bins >> 9)).astype(F32)
     w_ref[...] = (bins & 255).astype(F32)
-    a_ref[...] = area_ref[...].astype(F32)
+    a_ref[...], b_ref[...] = halves(area_ref[...].astype(F32))
     raw_ref[...] = jnp.zeros_like(raw_ref)
     cong_ref[...] = jnp.zeros_like(cong_ref)
     nil = jnp.zeros((), BF16)
     one = jnp.ones((), BF16)
     s_iota = narrow(sublane_iota(2 * TILE_R))
     w_iota = narrow(sublane_iota(256))
-
-    def cells(step, carry):
-        left, right = [], []
-        for k in range(GROUP):
-            r = step * GROUP + k
-            here = pl.ds(r, 1)
-            hit = s_iota == spread(s_ref[here, :], 2 * TILE_R)
-            left.append(jnp.where(hit, spread(a_ref[here, :], 2 * TILE_R), nil))
-            right.append(jnp.where(w_iota == spread(w_ref[here, :], 256), one, nil))
-        raw_ref[...] += dot_nt(jnp.concatenate(left, axis=1), jnp.concatenate(right, axis=1))
-        return carry
-
-    lax.fori_loop(0, bin_ref.shape[0] // GROUP, cells, 0)
-    width = GROUP * LANES
+    steps = 8
+    group = bin_ref.shape[0] // steps
+    width = box_ref.shape[1] // steps
     r_iota = narrow(sublane_iota(TILE_R, width))
     c_iota = narrow(sublane_iota(TILE_C, width) - TILE_C // 2)
 
-    def nets(step, carry):
-        box = box_ref[:, pl.ds(pl.multiple_of(step * width, width), width)].astype(F32)
+    def step(k, carry):
+        left, right = [], []
+        for j in range(group):
+            here = pl.ds(k * group + j, 1)
+            hit = s_iota == spread(s_ref[here, :], 2 * TILE_R)
+            left.append(
+                jnp.concatenate(
+                    [jnp.where(hit, spread(x[here, :], 2 * TILE_R), nil).astype(F8) for x in (a_ref, b_ref)], axis=0
+                )
+            )
+            right.append(jnp.where(w_iota == spread(w_ref[here, :], 256), one, nil).astype(F8))
+        raw_ref[...] += dot_nt(jnp.concatenate(left, axis=1), jnp.concatenate(right, axis=1))
+        box = box_ref[:, pl.ds(pl.multiple_of(k * width, width), width)].astype(F32)
         tall = box[1:2] - box[0:1] + 1.0
         wide = box[3:4] - box[2:3] + 1.0
-        weight = (tall + wide) / (tall * wide)
+        weight = ((tall + wide) / (tall * wide)).astype(BF16).astype(F32)
+        big, small = halves(weight)
         rows = (r_iota >= spread(box[0:1], TILE_R)) & (r_iota <= spread(box[1:2], TILE_R))
-        half = float(TILE_C // 2)
-        cols = (c_iota >= spread(box[2:3] - half, TILE_C)) & (c_iota <= spread(box[3:4] - half, TILE_C))
+        middle = float(TILE_C // 2)
+        cols = (c_iota >= spread(box[2:3] - middle, TILE_C)) & (c_iota <= spread(box[3:4] - middle, TILE_C))
         cong_ref[...] += dot_nt(
-            jnp.where(rows, one, nil), jnp.where(cols, spread(weight, TILE_C), nil)
+            jnp.where(cols, one, nil).astype(F8),
+            jnp.concatenate(
+                [jnp.where(rows, spread(x, TILE_R), nil).astype(F8) for x in (big, small * SMALL)], axis=0
+            ),
         )
         return carry
 
-    lax.fori_loop(0, box_ref.shape[1] // width, nets, 0)
-    raw = jnp.concatenate([raw_ref[:TILE_R], raw_ref[TILE_R:]], axis=1)
-    dens = raw * (1.0 + GAMMA * cong_ref[...])
+    lax.fori_loop(0, steps, step, 0)
+    raw = raw_ref[: 2 * TILE_R] + raw_ref[2 * TILE_R :]
+    raw = jnp.concatenate([raw[:TILE_R], raw[TILE_R:]], axis=1)
+    cong = cong_ref[...].T
+    cong = cong[:TILE_R] + cong[TILE_R:] * (1.0 / SMALL)
+    dens = raw * (1.0 + GAMMA * cong)
     dens_ref[...] = dens
     top_ref[...] = dens[:EDGE]
     bottom_ref[...] = dens[TILE_R - EDGE :]
@@ -104,11 +121,11 @@
             target[o, slot] = jnp.where(keep, jnp.where(near, a, b), fill)
         return carry
 
-    lax.fori_loop(0, parts, one_owner, 0)
+    lax.fori_loop(0, parts, one_owner, 0, unroll=8)
 
 
 def order_kernel(parts, owner_ref, bin_ref, area_ref, slots_ref, sorted_ref, starts_ref,
-                 pre_ref, cnt_ref, s_ref, w_ref, bh_ref, bl_ref, ar_ref, acc_ref, b_ref, a_ref, vec_ref, smem_ref, sem):
+                 pre_ref, cnt_ref, s_ref, w_ref, d2_ref, d1_ref, d0_ref, big_ref, small_ref, acc_ref, b_ref, a_ref, vec_ref, smem_ref, sem):
     rows = owner_ref.shape[0]
     i = sublane_iota(LANES, 2 * LANES)
     j = lax.broadcasted_iota(jnp.int32, (LANES, 2 * LANES), 1)
@@ -158,10 +175,14 @@
     top = jnp.where(dest >= half * LANES, 1, 0)
     s_ref[...] = ((dest >> 7) - top * half).astype(F32)
     w_ref[...] = ((dest & (LANES - 1)) + top * LANES).astype(F32)
-    bins = bin_ref[...]
-    bh_ref[...] = (bins >> 8).astype(F32)
-    bl_ref[...] = (bins & 255).astype(F32)
-    ar_ref[...] = area_ref[...].astype(F32)
+    bins = bin_ref[...] - MIDDLE
+    d0 = ((bins + 16) & 31) - 16
+    rest = (bins - d0) >> 5
+    d1 = ((rest + 16) & 31) - 16
+    d0_ref[...] = d0.astype(F32)
+    d1_ref[...] = d1.astype(F32)
+    d2_ref[...] = ((rest - d1) >> 5).astype(F32)
+    big_ref[...], small_ref[...] = halves(area_ref[...].astype(F32))
     acc_ref[...] = jnp.zeros_like(acc_ref)
     nil = jnp.zeros((), BF16)
     one = jnp.ones((), BF16)
@@ -175,10 +196,10 @@
             hit = s_iota == spread(s_ref[here, :], half)
             left.append(
                 jnp.concatenate(
-                    [jnp.where(hit, spread(x[here, :], half), nil) for x in (bh_ref, bl_ref, ar_ref)], axis=0
+                    [jnp.where(hit, spread(x[here, :], half), nil).astype(F8) for x in (d2_ref, d1_ref, d0_ref, big_ref, small_ref)], axis=0
                 )
             )
-            right.append(jnp.where(w_iota == spread(w_ref[here, :], 2 * LANES), one, nil))
+            right.append(jnp.where(w_iota == spread(w_ref[here, :], 2 * LANES), one, nil).astype(F8))
         acc_ref[...] += dot_nt(jnp.concatenate(left, axis=1), jnp.concatenate(right, axis=1))
         return carry
 
@@ -186,8 +207,9 @@
     for h in range(2):
         cols = slice(h * LANES, (h + 1) * LANES)
         out = slice(h * half, (h + 1) * half)
-        b_ref[out, :] = acc_ref[:half, cols] * 256.0 + acc_ref[half : 2 * half, cols]
-        a_ref[out, :] = acc_ref[2 * half :, cols]
+        part = [acc_ref[k * half : (k + 1) * half, cols] for k in range(5)]
+        b_ref[out, :] = (part[0] * 32.0 + part[1]) * 32.0 + part[2] + float(MIDDLE)
+        a_ref[out, :] = part[3] + part[4]
     pad = slice(rows, b_ref.shape[0])
     b_ref[pad, :] = jnp.zeros((b_ref.shape[0] - rows, LANES), F32)
     a_ref[pad, :] = jnp.zeros((b_ref.shape[0] - rows, LANES), F32)
@@ -197,7 +219,7 @@
 
 
 def flow_kernel(parts, grid_rows, grid_cols, starts_ref, place_ref, dens_in, up_ref, down_ref, left_ref, right_ref, sorted_ref,
-                dens_ref, slots_ref, pad_ref, hi_ref, lo_ref, row_ref, col_ref):
+                dens_ref, slots_ref, pad_ref, hi_ref, lo_ref, row_ref, col_ref, table_ref):
     rows = sorted_ref.shape[0]
     mid = pl.ds(EDGE, TILE_R)
     inner = pl.ds(LANES, TILE_C)
@@ -235,25 +257,43 @@
         fine.append((table - big.astype(F32)).astype(BF16))
     table = jnp.concatenate(coarse + fine, axis=0)
     bins = sorted_ref[...].astype(jnp.int32)
-    hi_ref[...] = (((bins >> 7) & 3) * TILE_R + (bins >> 9)).astype(F32)
-    lo_ref[...] = (bins & (LANES - 1)).astype(F32)
+    hi_ref[:rows] = (((bins >> 7) & 3) * TILE_R + (bins >> 9)).astype(F32)
+    lo_ref[:rows] = (bins & (LANES - 1)).astype(F32)
+    hi_ref[rows:] = jnp.zeros((hi_ref.shape[0] - rows, LANES), F32)
+    lo_ref[rows:] = jnp.zeros((hi_ref.shape[0] - rows, LANES), F32)
     hi_iota = narrow(sublane_iota(256))
     lo_iota = sublane_iota(LANES).astype(F32)
     nil = jnp.zeros((), BF16)
     one = jnp.ones((), BF16)
-    group = 8
+    for k in range(TILE_C // LANES):
+        cols = slice(k * LANES, (k + 1) * LANES)
+        out = slice(k * TILE_R, (k + 1) * TILE_R)
+        table_ref[0, out, :] = flow_row[:, cols]
+        table_ref[1, out, :] = flow_col[:, cols]
 
     def look_up(step, carry):
+        first = step * (DIRECT + BY_DOT)
+        here = pl.ds(first, DIRECT)
+        row_here, lane_here = hi_ref[here, :], lo_ref[here, :].astype(jnp.int32)
+        got = [jnp.zeros((DIRECT, LANES), F32)] * 2
+        for k in range(table_ref.shape[1]):
+            hit = row_here == float(k)
+            for c in range(2):
+                line = jnp.broadcast_to(table_ref[c, k : k + 1, :], (DIRECT, LANES))
+                near = jnp.take_along_axis(line, lane_here, axis=1, mode="promise_in_bounds")
+                got[c] = jnp.where(hit, near, got[c])
+        row_ref[here, :] = got[0]
+        col_ref[here, :] = got[1]
         picks = jnp.concatenate(
             [
-                jnp.where(hi_iota == spread(hi_ref[pl.ds(step * group + k, 1), :], 256), one, nil)
-                for k in range(group)
+                jnp.where(hi_iota == spread(hi_ref[pl.ds(first + DIRECT + k, 1), :], 256), one, nil)
+                for k in range(BY_DOT)
             ],
             axis=1,
         )
         found = jnp.dot(table, picks, preferred_element_type=F32)
-        for k in range(group):
-            here = pl.ds(step * group + k, 1)
+        for k in range(BY_DOT):
+            here = pl.ds(first + DIRECT + k, 1)
             hit = lo_iota == lo_ref[here, :]
             part = found[:, k * LANES : (k + 1) * LANES]
             both = part[: 2 * LANES] + part[2 * LANES :]
@@ -261,7 +301,7 @@
             col_ref[here, :] = jnp.sum(jnp.where(hit, both[LANES:], 0.0), axis=0, keepdims=True)
         return carry
 
-    lax.fori_loop(0, rows // group, look_up, 0)
+    lax.fori_loop(0, -(-rows // (DIRECT + BY_DOT)), look_up, 0)
     pad = slice(rows, row_ref.shape[0])
     row_ref[pad, :] = jnp.zeros((row_ref.shape[0] - rows, LANES), F32)
     col_ref[pad, :] = jnp.zeros((row_ref.shape[0] - rows, LANES), F32)
@@ -282,7 +322,7 @@
     rows = count // LANES
     capacity = 2 * count // parts
     per = capacity // LANES
-    spare = -(-(per + 1) // 8) * 8
+    spare = -(-max(per + 1, -rows % (DIRECT + BY_DOT)) // 8) * 8
     bins = cell_bin.reshape(rows, LANES)
     area = cell_area.reshape(rows, LANES)
     n_rows, n_cols = lax.axis_size("rows"), lax.axis_size("cols")
@@ -290,7 +330,7 @@
     dens, top, bottom = pl.pallas_call(
         density_kernel,
         out_shape=(shape(TILE_R, TILE_C), shape(EDGE, TILE_C), shape(EDGE, TILE_C)),
-        scratch_shapes=[vmem(rows, LANES)] * 3 + [vmem(2 * TILE_R, 256), vmem(TILE_R, TILE_C)],
+        scratch_shapes=[vmem(rows, LANES)] * 4 + [vmem(4 * TILE_R, 256), vmem(TILE_C, 2 * TILE_R)],
         name="density",
     )(bins, area, net_box)
     ahead = [(k, k + 1) for k in range(n_rows - 1)]
@@ -300,8 +340,8 @@
     slots, in_order, starts = pl.pallas_call(
         functools.partial(order_kernel, parts),
         out_shape=(shape(parts, 2, per, LANES), shape(rows, LANES), shape(8, LANES, dtype=jnp.int32)),
-        scratch_shapes=[vmem(rows, LANES)] * 7
-        + [vmem(3 * rows // 2, 2 * LANES), vmem(rows + spare, LANES), vmem(rows + spare, LANES),
+        scratch_shapes=[vmem(rows, LANES)] * 9
+        + [vmem(5 * rows // 2, 2 * LANES), vmem(rows + spare, LANES), vmem(rows + spare, LANES),
            vmem(8, LANES, dtype=jnp.int32), pltpu.SMEM((8, LANES), jnp.int32), pltpu.SemaphoreType.DMA],
         cost_estimate=pl.CostEstimate(flops=15_000_000_000, bytes_accessed=2_000_000, transcendentals=0),
         name="order",
@@ -319,8 +359,7 @@
         functools.partial(flow_kernel, parts, grid_rows, grid_cols),
         out_shape=(shape(TILE_R, TILE_C), shape(parts, 2, per, LANES)),
         in_specs=[scalars, scalars] + [whole] * 6,
-        scratch_shapes=[vmem(TILE_R + 2 * EDGE, TILE_C + 2 * LANES), vmem(rows, LANES), vmem(rows, LANES),
-                        vmem(rows + spare, LANES), vmem(rows + spare, LANES)],
+        scratch_shapes=[vmem(TILE_R + 2 * EDGE, TILE_C + 2 * LANES), *[vmem(rows + spare, LANES)] * 4, vmem(2, 256, LANES)],
         cost_estimate=pl.CostEstimate(flops=15_000_000_000, bytes_accessed=2_000_000, transcendentals=0),
         name="flow",
     )(starts, place, dens, up, down, left, right, in_order)

time: 100 us -> 81.3 us (0.81)
  Pallas kernels: 53.5 us -> 34.5 us
    pallas_call x1, Pallas kernels: 19.8 us -> 12.1 us  [on_device(): pl.pallas_call(functools.partial(flow_kernel, parts, grid_rows, grid_cols...]
    pallas_call x1, Pallas kernels: 15.6 us -> 9.33 us  [on_device(): pl.pallas_call(density_kernel, out_shape=(shape(TILE_R, TILE_C), shape(ED...]
    pallas_call x1, Pallas kernels: 18 us -> 13.1 us  [on_device(): pl.pallas_call(functools.partial(order_kernel, parts), out_shape=(shape(p...]
  transfers between devices with their start and end apart: 6 -> 6, of which waited for: 2 -> 2; matrix products, arithmetic and copies ran while one was open for 1% -> 2% of each run, Pallas kernels for 38% -> 31%
where the time goes in v2:
time: 81.3 us; the launch traced here: 80.8 us
  Pallas kernels  34.5 us (42%)
  starting transfers between devices  25.6 us (31%)
  waiting for transfers between devices  15.2 us (19%)
  other arithmetic  2.95 us (4%)
  local copies, waits for them, and re-layouts  1.81 us (2%)
    all_to_all x1, waiting for transfers between devices, on_device(): second = lax.all_to_all(shifts, ('rows', 'cols'), 0, 0, tiled=True)  14.9 us
    pallas_call x1, Pallas kernels, on_device(): pl.pallas_call(functools.partial(order_kernel, parts), out_shape=(shape(p...  13.1 us
    pallas_call x1, Pallas kernels, on_device(): pl.pallas_call(functools.partial(flow_kernel, parts, grid_rows, grid_cols...  12.1 us
    pallas_call x1, Pallas kernels, on_device(): pl.pallas_call(density_kernel, out_shape=(shape(TILE_R, TILE_C), shape(ED...  9.33 us
    all_to_all x1, starting transfers between devices, on_device(): second = lax.all_to_all(shifts, ('rows', 'cols'), 0, 0, tiled=True)  8.15 us
    all_to_all x1, starting transfers between devices, on_device(): first = lax.all_to_all(slots, ('rows', 'cols'), 0, 0, tiled=True)  7 us
    ppermute x1, starting transfers between devices, on_device(): up = lax.ppermute(bottom, 'rows', ahead)  4.86 us
    ppermute x1, starting transfers between devices, on_device(): left = lax.ppermute(strip[:, TILE_C - LANES:], 'cols', ahead)  3.03 us
  transfers between devices with their start and end apart: 6, of which 2 were waited for; matrix products, arithmetic and copies ran while one was open for 2% of the time, Pallas kernels for 31%

profile of v2, /device:TPU:0, one launch (start us, length us, event | category | flops | bytes accessed | tf_op | source)
XLA Modules:
  0.0 80.8 jit_solution(7098377717151281997)
XLA Ops:
  0.6 9.3 %density.1 = (f32[64,512]{1,0:T(8,128)}, f32[8,512]{1,0:T(8,128)}, f32[8,512]{1,0:T(8,128)}) custom-call(s32[256,128]{1,0:T(8,128)} %bitcast.13, bf16[256,128]{1,0:T(8,128)(2,1)} %bitcast.15, s32[4,16384]{1,0:T(4,128)} %box_ref.1), custom_call_target="tpu_custom_call" | custom-call | tf_op jit(solution)/shard_map/density/pallas_call | solution.py:330
  10.0 4.9 %collective-permute-start = (f32[8,512]{1,0:T(8,128)}, f32[8,512]{1,0:T(8,128)S(1)}, u32[]{:S(2)}, u32[]{:S(2)}) collective-permute-start(f32[8,512]{1,0:T(8,128)} %get-tuple-element.13), channel_id=1, source_target_pairs={{0,4},{4,8},{8,12},{12,16},{16,20},{20,24},{24,28},{1,5},{5,9},{9,... | collective-permute-start | bytes 49160 | tf_op jit(solution)/shard_map/ppermute | solution.py:338
  14.8 1.3 %collective-permute-start.1 = (f32[8,512]{1,0:T(8,128)}, f32[8,512]{1,0:T(8,128)S(1)}, u32[]{:S(2)}, u32[]{:S(2)}) collective-permute-start(f32[8,512]{1,0:T(8,128)} %get-tuple-element.14), channel_id=1, source_target_pairs={{4,0},{8,4},{12,8},{16,12},{20,16},{24,20},{28,24},{5,1},{9,5},{13... | collective-permute-start | bytes 49160 | tf_op jit(solution)/shard_map/ppermute | solution.py:339
  16.1 13.1 %order.1 = (f32[32,2,16,128]{3,2,1,0:T(8,128)}, f32[256,128]{1,0:T(8,128)}, s32[8,128]{1,0:T(8,128)}) custom-call(s32[256,128]{1,0:T(8,128)} %bitcast.17, s32[256,128]{1,0:T(8,128)} %bitcast.14, bf16[256,128]{1,0:T(8,128)(2,1)} %bitcast.16), custom_call_target="tpu_custom_call" | custom-call | flops 15000000512 | bytes 2000000 | tf_op jit(solution)/shard_map/order/pallas_call | solution.py:340
  29.2 0.0 copy-start
  29.2 7.0 %all-to-all-start.1 = ((f32[32,2,16,128]{3,2,1,0:T(8,128)}), f32[32,2,16,128]{3,2,1,0:T(8,128)S(1)}, u32[]{:S(2)}, u32[]{:S(2)}) async-start(f32[32,2,16,128]{3,2,1,0:T(8,128)} %get-tuple-element.18), calls=%async_computation.1 | async-start | bytes 1048576 | tf_op jit(solution)/shard_map/all_to_all | solution.py:354
  36.2 0.0 collective-permute-done.up_ref
  36.2 0.0 copy-start.1
  36.2 0.6 copy-done.1
  36.8 0.0 copy-done
  36.8 0.0 collective-permute-done.1.down_ref
  36.9 0.0 copy-start.2
  36.9 0.6 copy-done.2
  37.5 1.3 %collective-permute-start.3 = (f32[80,128]{1,0:T(8,128)S(1)}, f32[80,128]{1,0:T(8,128)S(1)}, u32[]{:S(2)}, u32[]{:S(2)}) collective-permute-start(f32[80,128]{1,0:T(8,128)S(1)} %get-tuple-element.23), channel_id=1, source_target_pairs={{1,0},{2,1},{3,2},{5,4},{6,5},{7,6},{9,8},{10,9},{11,10},{13,12},{... | collective-permute-start | bytes 122888 | tf_op jit(solution)/shard_map/ppermute | solution.py:353
  38.7 3.0 %collective-permute-start.2 = (f32[80,128]{1,0:T(8,128)S(1)}, f32[80,128]{1,0:T(8,128)S(1)}, u32[]{:S(2)}, u32[]{:S(2)}) collective-permute-start(f32[80,128]{1,0:T(8,128)S(1)} %get-tuple-element.24), channel_id=1, source_target_pairs={{0,1},{1,2},{2,3},{4,5},{5,6},{6,7},{8,9},{9,10},{10,11},{12,13},{... | collective-permute-start | bytes 122888 | tf_op jit(solution)/shard_map/ppermute | solution.py:352
  41.8 0.6 pad_add_fusion.place_ref
  42.3 0.0 collective-permute-done.3.right_ref
  42.3 0.0 copy-start.3
  42.3 0.3 collective-permute-done.2.left_ref
  42.6 0.0 copy-start.4
  42.6 0.3 copy-done.3
  43.0 0.3 copy-done.4
  43.2 12.1 %flow.1 = (f32[64,512]{1,0:T(8,128)}, f32[32,2,16,128]{3,2,1,0:T(8,128)}) custom-call(s32[8,128]{1,0:T(8,128)} %get-tuple-element.11.starts_ref, s32[2]{0:T(128)} %pad_add_fusion.place_ref, f32[64,512]{1,0:T(8,128)} %get-tuple-element.12.dens_in, f32[8,512]{1,0:T(8,128)} %copy-done.1, f32[8,512]{1,0:T(8,128)} %copy-done.2, f32[80,128]{1,0:T(8,128)} %copy-done.4, ...), custom_call_target="tpu_custom_call" | custom-call | flops 15000000512 | bytes 2000000 | tf_op jit(solution)/shard_map/flow/pallas_call | solution.py:358
  55.3 0.0 all-to-all-done.1
  55.4 8.1 %all-to-all-start = ((f32[32,2,16,128]{3,2,1,0:T(8,128)}), f32[32,2,16,128]{3,2,1,0:T(8,128)S(1)}, u32[]{:S(2)}, u32[]{:S(2)}) async-start(f32[32,2,16,128]{3,2,1,0:T(8,128)} %get-tuple-element.17), calls=%async_computation | async-start | bytes 1048576 | tf_op jit(solution)/shard_map/all_to_all | solution.py:366
  63.5 0.7 slice_convert_fusion
  64.3 14.9 %all-to-all-done = f32[32,2,16,128]{3,2,1,0:T(8,128)S(1)} async-done(((f32[32,2,16,128]{3,2,1,0:T(8,128)}), f32[32,2,16,128]{3,2,1,0:T(8,128)S(1)}, u32[]{:S(2)}, u32[]{:S(2)}) %all-to-all-start) | async-done | bytes 524320 | tf_op jit(solution)/shard_map/all_to_all | solution.py:366
  79.2 1.6 %pad_maximum_fusion = f32[3,65536]{1,0:T(4,128)} fusion(f32[1,65536]{1,0:T(1,128)S(1)} %bitcast.9, f32[1,65536]{1,0:T(1,128)S(1)} %bitcast.11, f32[1,65536]{1,0:T(1,128)S(1)} %bitcast.10), kind=kLoop, calls=%fused_computation | loop fusion | flops 393216 | bytes 1572864 | tf_op jit(solution)/shard_map/stack | solution.py:367
  (5 shorter events, 0.1 us)
Async XLA Ops:
  10.0 26.3 %collective-permute-start = (f32[8,512]{1,0:T(8,128)}, f32[8,512]{1,0:T(8,128)S(1)}, u32[]{:S(2)}, u32[]{:S(2)}) collective-permute-start(f32[8,512]{1,0:T(8,128)} %get-tuple-element.13), channel_id=1, source_target_pairs={{0,4},{4,8},{8,12},{12,16},{16,20},{20,24},{24,28},{1,5},{5,9},{9,... | collective-permute-start | bytes 49160 | tf_op jit(solution)/shard_map/ppermute | solution.py:338
  14.8 22.0 %collective-permute-start.1 = (f32[8,512]{1,0:T(8,128)}, f32[8,512]{1,0:T(8,128)S(1)}, u32[]{:S(2)}, u32[]{:S(2)}) collective-permute-start(f32[8,512]{1,0:T(8,128)} %get-tuple-element.14), channel_id=1, source_target_pairs={{4,0},{8,4},{12,8},{16,12},{20,16},{24,20},{28,24},{5,1},{9,5},{13... | collective-permute-start | bytes 49160 | tf_op jit(solution)/shard_map/ppermute | solution.py:339
  29.2 7.6 %copy-start = (f32[64,512]{1,0:T(8,128)S(1)}, f32[64,512]{1,0:T(8,128)}, u32[]{:S(2)}) copy-start(f32[64,512]{1,0:T(8,128)} %get-tuple-element.12.dens_in) | copy-start | bytes 393220
  29.2 26.2 %all-to-all-start.1 = ((f32[32,2,16,128]{3,2,1,0:T(8,128)}), f32[32,2,16,128]{3,2,1,0:T(8,128)S(1)}, u32[]{:S(2)}, u32[]{:S(2)}) async-start(f32[32,2,16,128]{3,2,1,0:T(8,128)} %get-tuple-element.18), calls=%async_computation.1 | async-start | bytes 1048576 | tf_op jit(solution)/shard_map/all_to_all | solution.py:354
  36.2 0.6 copy-start.1
  36.9 0.6 copy-start.2
  37.5 4.9 %collective-permute-start.3 = (f32[80,128]{1,0:T(8,128)S(1)}, f32[80,128]{1,0:T(8,128)S(1)}, u32[]{:S(2)}, u32[]{:S(2)}) collective-permute-start(f32[80,128]{1,0:T(8,128)S(1)} %get-tuple-element.23), channel_id=1, source_target_pairs={{1,0},{2,1},{3,2},{5,4},{6,5},{7,6},{9,8},{10,9},{11,10},{13,12},{... | collective-permute-start | bytes 122888 | tf_op jit(solution)/shard_map/ppermute | solution.py:353
  38.7 3.9 %collective-permute-start.2 = (f32[80,128]{1,0:T(8,128)S(1)}, f32[80,128]{1,0:T(8,128)S(1)}, u32[]{:S(2)}, u32[]{:S(2)}) collective-permute-start(f32[80,128]{1,0:T(8,128)S(1)} %get-tuple-element.24), channel_id=1, source_target_pairs={{0,1},{1,2},{2,3},{4,5},{5,6},{6,7},{8,9},{9,10},{10,11},{12,13},{... | collective-permute-start | bytes 122888 | tf_op jit(solution)/shard_map/ppermute | solution.py:352
  42.3 0.6 copy-start.3
  42.6 0.6 copy-start.4
  55.4 23.8 %all-to-all-start = ((f32[32,2,16,128]{3,2,1,0:T(8,128)}), f32[32,2,16,128]{3,2,1,0:T(8,128)S(1)}, u32[]{:S(2)}, u32[]{:S(2)}) async-start(f32[32,2,16,128]{3,2,1,0:T(8,128)} %get-tuple-element.17), calls=%async_computation | async-start | bytes 1048576 | tf_op jit(solution)/shard_map/all_to_all | solution.py:366

commit v3 on v2

v3 whole, which is shorter than its diff:
```python
import functools
import jax
import jax.numpy as jnp
from jax import lax
from jax.experimental import pallas as pl
from jax.experimental.pallas import tpu as pltpu
from jax.sharding import PartitionSpec as P

TILE_R = 64
TILE_C = 512
DIFF_STEPS = 4
RATE = 0.2
GAMMA = 0.05
LANES = 128
EDGE = 8
DIRECT = 8
BY_DOT = 12
BF16 = jnp.bfloat16
F8 = jnp.float8_e4m3fn
SMALL = 64.0
SYMBOLS = 119
GRANT = 24 * 2 ** 20
BASE = 233
F32 = jnp.float32


def dot_nt(a, b):
    return lax.dot_general(a, b, (((1,), (1,)), ((), ())), preferred_element_type=F32)


def sublane_iota(rows, lanes=LANES):
    return lax.broadcasted_iota(jnp.int32, (rows, lanes), 0)


def narrow(x):
    return x.astype(F32).astype(BF16)


def spread(row, rows):
    lanes = row.shape[1]
    packed = jnp.broadcast_to(row, (16, lanes)).astype(BF16)
    return jnp.broadcast_to(packed[None], (rows // 16, 16, lanes)).reshape(rows, lanes)


def halves(x):
    big = x.astype(F8).astype(F32)
    return big, x - big


def expand(parts, starts_ref, total, pairs):
    per = pairs[0][2].shape[-2]
    lane = lax.broadcasted_iota(jnp.int32, (per, LANES), 1)
    place = sublane_iota(per) * LANES + lane

    def one_owner(o, carry):
        start = starts_ref[0, o]
        stop = jnp.where(o + 1 < parts, starts_ref[0, jnp.minimum(o + 1, parts - 1)], total)
        row = start // LANES
        shift = start - row * LANES
        back = lax.rem(LANES - shift, LANES)
        keep = place < stop - start
        near = lane < LANES - shift
        for source, slot, target, fill in pairs:
            a = pltpu.roll(source[pl.ds(row, per), :], back, 1)
            b = pltpu.roll(source[pl.ds(row + 1, per), :], back, 1)
            target[o, slot] = jnp.where(keep, jnp.where(near, a, b), fill)
        return carry

    lax.fori_loop(0, parts, one_owner, 0, unroll=8)


def divide(x, base):
    guess = (x.astype(F32) * (1.0 / base)).astype(jnp.int32)
    rest = x - guess * base
    guess = guess + jnp.where(rest >= base, 1, 0) - jnp.where(rest < 0, 1, 0)
    return guess, x - guess * base


def symbol(digit):
    low = digit < SYMBOLS
    j = jnp.where(low, digit, digit - SYMBOLS)
    size = jnp.left_shift(8 + (j & 7), j >> 3).astype(F32) * (1.0 / 512.0)
    return jnp.where(low, size, -size)


def digit_of(value):
    size = (jnp.abs(value) * 512.0).astype(jnp.int32)
    scale = 28 - lax.clz(size)
    j = scale * 8 + jnp.right_shift(size, scale) - 8
    return jnp.where(value < 0.0, j + SYMBOLS, j)


def area_code(area):
    return jnp.where(
        area < 1.0,
        (area - 0.5) * 256.0,
        jnp.where(area < 2.0, (area - 1.0) * 128.0 + 128.0, (area - 2.0) * 64.0 + 256.0),
    ).astype(jnp.int32)


def area_of(code):
    x = code.astype(F32)
    return jnp.where(
        x < 128.0, x * (1.0 / 256.0) + 0.5, jnp.where(x < 256.0, x * (1.0 / 128.0), x * (1.0 / 64.0) - 2.0)
    )


def placed(refs, s_ref, w_ref, first, group):
    nil = jnp.zeros((), BF16)
    one = jnp.ones((), BF16)
    s_iota = narrow(sublane_iota(LANES))
    w_iota = narrow(sublane_iota(2 * LANES))
    left, right = [], []
    for j in range(group):
        here = pl.ds(first + j, 1)
        hit = s_iota == spread(s_ref[here, :], LANES)
        left.append(
            jnp.concatenate([jnp.where(hit, spread(x[here, :], LANES), nil).astype(F8) for x in refs], axis=0)
        )
        right.append(jnp.where(w_iota == spread(w_ref[here, :], 2 * LANES), one, nil).astype(F8))
    return dot_nt(jnp.concatenate(left, axis=1), jnp.concatenate(right, axis=1))


STEPS = 8


def before(lanes):
    return narrow(sublane_iota(LANES, lanes) < lax.broadcasted_iota(jnp.int32, (LANES, lanes), 1))


def density_kernel(parts, bin_ref, area_ref, box_ref, owner_ref, dens_ref, top_ref, bottom_ref, pre_ref, cnt_ref,
                   s_ref, w_ref, a_ref, b_ref, raw_ref, cong_ref):
    all_rows = bin_ref.shape[0]
    bins = bin_ref[...]
    area = area_ref[...].astype(F32)
    s_ref[...] = (((bins >> 8) & 1) * TILE_R + (bins >> 9)).astype(F32)
    w_ref[...] = (bins & 255).astype(F32)
    a_ref[...], b_ref[...] = halves(area)
    raw_ref[...] = jnp.zeros_like(raw_ref)
    cong_ref[...] = jnp.zeros_like(cong_ref)
    nil = jnp.zeros((), BF16)
    one = jnp.ones((), BF16)
    steps = STEPS
    group = all_rows // steps
    width = box_ref.shape[1] // steps
    r_iota = narrow(sublane_iota(TILE_R, width))
    c_iota = narrow(sublane_iota(TILE_C, width) - TILE_C // 2)
    upper = before(2 * LANES)
    lane = lax.broadcasted_iota(jnp.int32, (group, LANES), 1)
    many = 8

    def step(k, carry):
        raw_ref[...] += placed((a_ref, b_ref), s_ref, w_ref, k * group, group)
        box = box_ref[:, pl.ds(pl.multiple_of(k * width, width), width)].astype(F32)
        tall = box[1:2] - box[0:1] + 1.0
        wide = box[3:4] - box[2:3] + 1.0
        weight = ((tall + wide) / (tall * wide)).astype(BF16).astype(F32)
        big, small = halves(weight)
        rows = (r_iota >= spread(box[0:1], TILE_R)) & (r_iota <= spread(box[1:2], TILE_R))
        middle = float(TILE_C // 2)
        cols = (c_iota >= spread(box[2:3] - middle, TILE_C)) & (c_iota <= spread(box[3:4] - middle, TILE_C))
        cong_ref[...] += dot_nt(
            jnp.where(cols, one, nil).astype(F8),
            jnp.concatenate(
                [jnp.where(rows, spread(x, TILE_R), nil).astype(F8) for x in (big, small * SMALL)], axis=0
            ),
        )
        here = pl.ds(pl.multiple_of(k * group, group), group)
        owner = owner_ref[here, :]
        prefix = jnp.zeros((group, LANES), F32)
        counts = jnp.zeros((group, LANES), F32)
        for g in range(0, parts, many):
            hits = [owner == g + m for m in range(many)]
            sums = jnp.dot(jnp.concatenate([narrow(h) for h in hits], axis=0), upper, preferred_element_type=F32)
            for m in range(many):
                part = sums[m * group : (m + 1) * group]
                prefix = jnp.where(hits[m], part[:, :LANES], prefix)
                counts = jnp.where(lane == g + m, part[:, LANES:], counts)
        pre_ref[here, :] = prefix
        cnt_ref[here, :] = counts
        return carry

    lax.fori_loop(0, steps, step, 0)
    raw = raw_ref[:LANES] + raw_ref[LANES:]
    raw = jnp.concatenate([raw[:TILE_R], raw[TILE_R:]], axis=1)
    cong = cong_ref[...].T
    cong = cong[:TILE_R] + cong[TILE_R:] * (1.0 / SMALL)
    dens = raw * (1.0 + GAMMA * cong)
    dens_ref[...] = dens
    top_ref[...] = dens[:EDGE]
    bottom_ref[...] = dens[TILE_R - EDGE :]


def order_kernel(parts, bin_ref, area_ref, owner_ref, pre_ref, cnt_ref, slots_ref, sorted_ref, starts_ref,
                 s_ref, w_ref, a_ref, b_ref, c_ref, acc_ref, run_bin_ref, run_area_ref, vec_ref, smem_ref, sem):
    all_rows = bin_ref.shape[0]
    group = all_rows // STEPS
    counts = cnt_ref[...]
    lower = narrow(
        lax.broadcasted_iota(jnp.int32, (all_rows, all_rows), 1)
        < lax.broadcasted_iota(jnp.int32, (all_rows, all_rows), 0)
    )
    base = jnp.dot(lower, counts.astype(BF16), preferred_element_type=F32)
    total = base[all_rows - 8 :] + counts[all_rows - 8 :]
    high = jnp.floor(total * (1.0 / 64.0))
    low = total - high * 64.0
    strict = before(LANES)
    first = jnp.dot(low.astype(BF16), strict, preferred_element_type=F32) + 64.0 * jnp.dot(
        high.astype(BF16), strict, preferred_element_type=F32
    )
    starts = jnp.broadcast_to(first[7:8], (8, LANES))
    vec_ref[...] = starts.astype(jnp.int32)
    starts_ref[...] = starts.astype(jnp.int32)
    copy = pltpu.make_async_copy(vec_ref, smem_ref, sem)
    copy.start()
    dest = (pre_ref[...] + jnp.take_along_axis(base + starts[:1], owner_ref[...], axis=1)).astype(jnp.int32)
    half = all_rows // 2
    top = jnp.where(dest >= half * LANES, 1, 0)
    s_ref[...] = ((dest >> 7) - top * half).astype(F32)
    w_ref[...] = ((dest & (LANES - 1)) + top * LANES).astype(F32)
    rest, digit = divide(area_code(area_ref[...].astype(F32)) * (TILE_R * TILE_C) + bin_ref[...], BASE)
    c_ref[...] = symbol(digit)
    rest, digit = divide(rest, BASE)
    b_ref[...] = symbol(digit)
    a_ref[...] = symbol(rest)
    acc_ref[...] = jnp.zeros_like(acc_ref)

    def place(k, carry):
        acc_ref[...] += placed((a_ref, b_ref, c_ref), s_ref, w_ref, k * group, group)
        return carry

    lax.fori_loop(0, STEPS, place, 0)
    for h in range(2):
        out = slice(h * half, (h + 1) * half)
        digits = [
            digit_of(acc_ref[k * half : (k + 1) * half, h * LANES : (h + 1) * LANES]) for k in range(3)
        ]
        code = (digits[0] * BASE + digits[1]) * BASE + digits[2]
        bins = code & (TILE_R * TILE_C - 1)
        sorted_ref[out, :] = bins
        run_bin_ref[out, :] = bins.astype(F32)
        run_area_ref[out, :] = area_of(code >> 15)
    pad = slice(all_rows, run_bin_ref.shape[0])
    run_bin_ref[pad, :] = jnp.zeros((run_bin_ref.shape[0] - all_rows, LANES), F32)
    run_area_ref[pad, :] = jnp.zeros((run_bin_ref.shape[0] - all_rows, LANES), F32)
    copy.wait()
    expand(parts, smem_ref, all_rows * LANES, ((run_bin_ref, 0, slots_ref, -1.0), (run_area_ref, 1, slots_ref, 0.0)))


def flow_kernel(parts, grid_rows, grid_cols, starts_ref, dens_in, up_ref, down_ref, left_ref, right_ref, sorted_ref,
                dens_ref, slots_ref, pad_ref, hi_ref, lo_ref, row_ref, col_ref, table_ref):
    rows = sorted_ref.shape[0]
    mid = pl.ds(EDGE, TILE_R)
    inner = pl.ds(LANES, TILE_C)
    pad_ref[mid, inner] = dens_in[...]
    pad_ref[:EDGE, inner] = up_ref[...]
    pad_ref[TILE_R + EDGE :, inner] = down_ref[...]
    pad_ref[:, :LANES] = left_ref[...]
    pad_ref[:, LANES + TILE_C :] = right_ref[...]
    tall, wide = pad_ref.shape
    grow = lax.axis_index("rows") * TILE_R + lax.broadcasted_iota(jnp.int32, (tall, 1), 0) - EDGE
    gcol = lax.axis_index("cols") * TILE_C + lax.broadcasted_iota(jnp.int32, (1, wide), 1) - LANES
    open_lower = grow + 1 != grid_rows
    open_upper = grow != 0
    open_right = gcol + 1 != grid_cols
    open_left = gcol != 0
    flow_row = jnp.zeros((TILE_R, TILE_C), F32)
    flow_col = jnp.zeros((TILE_R, TILE_C), F32)
    for step in range(DIFF_STEPS):
        d = pad_ref[...]
        lower = jnp.where(open_lower, pltpu.roll(d, tall - 1, 0) - d, 0.0)
        upper = jnp.where(open_upper, pltpu.roll(d, 1, 0) - d, 0.0)
        right = jnp.where(open_right, pltpu.roll(d, wide - 1, 1) - d, 0.0)
        left = jnp.where(open_left, pltpu.roll(d, 1, 1) - d, 0.0)
        pad_ref[...] = d + RATE * ((lower + upper) + (right + left))
        centre = (slice(EDGE, EDGE + TILE_R), slice(LANES, LANES + TILE_C))
        rate = -0.5 / (d[centre] + 1.0)
        flow_row += (lower - upper)[centre] * rate
        flow_col += (right - left)[centre] * rate
    dens_ref[...] = pad_ref[mid, inner]
    coarse, fine = [], []
    for flow in (flow_row, flow_col):
        table = jnp.concatenate([flow[:, k * LANES : (k + 1) * LANES] for k in range(TILE_C // LANES)], axis=0).T
        big = table.astype(BF16)
        coarse.append(big)
        fine.append((table - big.astype(F32)).astype(BF16))
    table = jnp.concatenate(coarse + fine, axis=0)
    bins = sorted_ref[...]
    hi_ref[:rows] = (((bins >> 7) & 3) * TILE_R + (bins >> 9)).astype(F32)
    lo_ref[:rows] = (bins & (LANES - 1)).astype(F32)
    hi_ref[rows:] = jnp.zeros((hi_ref.shape[0] - rows, LANES), F32)
    lo_ref[rows:] = jnp.zeros((hi_ref.shape[0] - rows, LANES), F32)
    hi_iota = narrow(sublane_iota(256))
    lo_iota = sublane_iota(LANES).astype(F32)
    nil = jnp.zeros((), BF16)
    one = jnp.ones((), BF16)
    for k in range(TILE_C // LANES):
        cols = slice(k * LANES, (k + 1) * LANES)
        out = slice(k * TILE_R, (k + 1) * TILE_R)
        table_ref[0, out, :] = flow_row[:, cols]
        table_ref[1, out, :] = flow_col[:, cols]

    def look_up(step, carry):
        first = step * (DIRECT + BY_DOT)
        here = pl.ds(first, DIRECT)
        row_here, lane_here = hi_ref[here, :], lo_ref[here, :].astype(jnp.int32)
        got = [jnp.zeros((DIRECT, LANES), F32)] * 2
        for k in range(table_ref.shape[1]):
            hit = row_here == float(k)
            for c in range(2):
                line = jnp.broadcast_to(table_ref[c, k : k + 1, :], (DIRECT, LANES))
                near = jnp.take_along_axis(line, lane_here, axis=1, mode="promise_in_bounds")
                got[c] = jnp.where(hit, near, got[c])
        row_ref[here, :] = got[0]
        col_ref[here, :] = got[1]
        picks = jnp.concatenate(
            [
                jnp.where(hi_iota == spread(hi_ref[pl.ds(first + DIRECT + k, 1), :], 256), one, nil)
                for k in range(BY_DOT)
            ],
            axis=1,
        )
        found = jnp.dot(table, picks, preferred_element_type=F32)
        for k in range(BY_DOT):
            here = pl.ds(first + DIRECT + k, 1)
            hit = lo_iota == lo_ref[here, :]
            part = found[:, k * LANES : (k + 1) * LANES]
            both = part[: 2 * LANES] + part[2 * LANES :]
            row_ref[here, :] = jnp.sum(jnp.where(hit, both[:LANES], 0.0), axis=0, keepdims=True)
            col_ref[here, :] = jnp.sum(jnp.where(hit, both[LANES:], 0.0), axis=0, keepdims=True)
        return carry

    lax.fori_loop(0, -(-rows // (DIRECT + BY_DOT)), look_up, 0)
    pad = slice(rows, row_ref.shape[0])
    row_ref[pad, :] = jnp.zeros((row_ref.shape[0] - rows, LANES), F32)
    col_ref[pad, :] = jnp.zeros((row_ref.shape[0] - rows, LANES), F32)
    expand(parts, starts_ref, rows * LANES, ((row_ref, 0, slots_ref, 0.0), (col_ref, 1, slots_ref, 0.0)))


def merge_kernel(first_ref, second_ref, out_ref, bin_ref):
    parts, _, per, _ = first_ref.shape

    def one_source(k, carry):
        bin_ref[pl.ds(pl.multiple_of(k * per, per), per), :] = first_ref[k, 0].astype(jnp.int32)
        for r in range(per):
            row = slice(r, r + 1)
            cells = jnp.concatenate([second_ref[k, 0, row, :], second_ref[k, 1, row, :], first_ref[k, 1, row, :]], axis=0)
            out_ref[:, pl.ds(pl.multiple_of((k * per + r) * LANES, LANES), LANES)] = cells
        return carry

    lax.fori_loop(0, parts, one_source, 0)


def shape(*dims, dtype=F32):
    return jax.ShapeDtypeStruct(dims, dtype)


def vmem(*dims, dtype=F32):
    return pltpu.VMEM(dims, dtype)


def on_device(cell_bin, cell_area, owner, net_box):
    parts = lax.axis_size(("rows", "cols"))
    count = cell_bin.shape[0]
    rows = count // LANES
    capacity = 2 * count // parts
    per = capacity // LANES
    spare = -(-max(per + 1, -rows % (DIRECT + BY_DOT)) // 8) * 8
    bins = cell_bin.reshape(rows, LANES)
    area = cell_area.reshape(rows, LANES)
    n_rows, n_cols = lax.axis_size("rows"), lax.axis_size("cols")
    grid_rows, grid_cols = n_rows * TILE_R, n_cols * TILE_C
    owner = owner.reshape(rows, LANES)
    cells = vmem(rows, LANES)
    runs = vmem(rows + spare, LANES)
    table = shape(rows, LANES)
    grant = pltpu.CompilerParams(vmem_limit_bytes=GRANT)
    dens, top, bottom, prefix, counts = pl.pallas_call(
        functools.partial(density_kernel, parts),
        out_shape=(shape(TILE_R, TILE_C), shape(EDGE, TILE_C), shape(EDGE, TILE_C), table, table),
        scratch_shapes=[cells] * 4 + [vmem(2 * LANES, 2 * LANES), vmem(TILE_C, 2 * TILE_R)],
        name="density",
    )(bins, area, net_box, owner)
    ahead = [(k, k + 1) for k in range(n_rows - 1)]
    behind = [(k + 1, k) for k in range(n_rows - 1)]
    up = lax.ppermute(bottom, "rows", ahead)
    down = lax.ppermute(top, "rows", behind)
    slots, in_order, starts = pl.pallas_call(
        functools.partial(order_kernel, parts),
        out_shape=(shape(parts, 2, per, LANES), shape(rows, LANES, dtype=jnp.int32), shape(8, LANES, dtype=jnp.int32)),
        scratch_shapes=[cells] * 5 + [vmem(3 * LANES, 2 * LANES), runs, runs]
        + [vmem(8, LANES, dtype=jnp.int32), pltpu.SMEM((8, LANES), jnp.int32), pltpu.SemaphoreType.DMA],
        compiler_params=grant,
        cost_estimate=pl.CostEstimate(flops=15_000_000_000, bytes_accessed=2_000_000, transcendentals=0),
        name="order",
    )(bins, area, owner, prefix, counts)
    up, down, slots = lax.optimization_barrier((up, down, slots))
    strip = jnp.concatenate([up, dens, down], axis=0)
    ahead = [(k, k + 1) for k in range(n_cols - 1)]
    behind = [(k + 1, k) for k in range(n_cols - 1)]
    left = lax.ppermute(strip[:, TILE_C - LANES :], "cols", ahead)
    right = lax.ppermute(strip[:, :LANES], "cols", behind)
    first = lax.all_to_all(slots, ("rows", "cols"), 0, 0, tiled=True)
    scalars = pl.BlockSpec(memory_space=pltpu.SMEM)
    density, shifts = pl.pallas_call(
        functools.partial(flow_kernel, parts, grid_rows, grid_cols),
        out_shape=(shape(TILE_R, TILE_C), shape(parts, 2, per, LANES)),
        in_specs=[scalars] + [pl.BlockSpec()] * 6,
        scratch_shapes=[vmem(TILE_R + 2 * EDGE, TILE_C + 2 * LANES), *[vmem(rows + spare, LANES)] * 4, vmem(2, 256, LANES)],
        compiler_params=grant,
        cost_estimate=pl.CostEstimate(flops=15_000_000_000, bytes_accessed=2_000_000, transcendentals=0),
        name="flow",
    )(starts, dens, up, down, left, right, in_order)
    second = lax.all_to_all(shifts, ("rows", "cols"), 0, 0, tiled=True)
    if per % 8:
        migrated = jnp.stack([second[:, 0].reshape(-1), second[:, 1].reshape(-1), first[:, 1].reshape(-1)])
        return density, migrated, first[:, 0].reshape(-1).astype(jnp.int32)
    migrated, migrated_bin = pl.pallas_call(
        merge_kernel,
        out_shape=(shape(3, parts * capacity), shape(parts * per, LANES, dtype=jnp.int32)),
        compiler_params=grant,
        name="merge",
    )(first, second)
    return density, migrated, migrated_bin.reshape(-1)


def solution(mesh):
    both = ("rows", "cols")
    in_specs = (P(both), P(both), P(both), P(None, both))
    out_specs = (P("rows", "cols"), P(None, both), P(both))
    return jax.shard_map(on_device, mesh=mesh, in_specs=in_specs, out_specs=out_specs, check_vma=False)
```

time: 81.3 us -> 74.4 us (0.915)
  blocking collectives: 0 us -> 18.4 us
  waiting for transfers between devices: 15.2 us -> 4.04 us
  starting transfers between devices: 25.6 us -> 17.5 us
  Pallas kernels: 34.5 us -> 31.5 us
  other arithmetic: 2.95 us -> 0 us
    all_to_all x0 -> x1, blocking collectives: none -> 18.4 us  [on_device(): second = lax.all_to_all(shifts, ('rows', 'cols'), 0, 0, tiled=True)]
    all_to_all x1 -> x0, waiting for transfers between devices: 14.9 us -> none  [on_device(): second = lax.all_to_all(shifts, ('rows', 'cols'), 0, 0, tiled=True)]
    all_to_all x1 -> x0, starting transfers between devices: 8.15 us -> none  [on_device(): second = lax.all_to_all(shifts, ('rows', 'cols'), 0, 0, tiled=True)]
    pallas_call x1, Pallas kernels: 13.1 us -> 7.12 us  [on_device(): pl.pallas_call(functools.partial(order_kernel, parts), out_shape=(shape(p...]
    all_to_all x1, waiting for transfers between devices: 0.01 us -> 4.03 us  [on_device(): first = lax.all_to_all(slots, ('rows', 'cols'), 0, 0, tiled=True)]
    pallas_call x1 -> x2, Pallas kernels: 9.33 us -> 12.8 us  [the longest x1 10.9 us: on_device(): pl.pallas_call(functools.partial(density_kernel, parts), out_shape=(shape...]
    another operation x2 -> x0, other arithmetic: 2.21 us -> none  [the longest x1 1.65 us: on_device(): jnp.stack([second[:, 0].reshape(-1), second[:, 1].reshape(-1), first[:, 1...]
    unnamed x12 -> x14, local copies, waits for them, and re-layouts: 1.77 us -> 1.83 us
  transfers between devices with their start and end apart: 6 -> 5, of which waited for: 2 -> 1; matrix products, arithmetic and copies ran while one was open for 2% -> 0% of each run, Pallas kernels for 31% -> 25%
where the time goes in v3:
time: 74.4 us; the launch traced here: 74.1 us
  Pallas kernels  31.5 us (42%)
  blocking collectives  18.4 us (25%)
  starting transfers between devices  17.5 us (24%)
  waiting for transfers between devices  4.04 us (5%)
  local copies, waits for them, and re-layouts  1.85 us (2%)
  between operations  0.81 us (1%)
    all_to_all x1, blocking collectives, on_device(): second = lax.all_to_all(shifts, ('rows', 'cols'), 0, 0, tiled=True)  18.4 us
    pallas_call x1, Pallas kernels, on_device(): pl.pallas_call(functools.partial(flow_kernel, parts, grid_rows, grid_cols...  11.6 us
    pallas_call x1, Pallas kernels, on_device(): pl.pallas_call(functools.partial(density_kernel, parts), out_shape=(shape...  10.9 us
    pallas_call x1, Pallas kernels, on_device(): pl.pallas_call(functools.partial(order_kernel, parts), out_shape=(shape(p...  7.12 us
    all_to_all x1, starting transfers between devices, on_device(): first = lax.all_to_all(slots, ('rows', 'cols'), 0, 0, tiled=True)  7.01 us
    ppermute x1, starting transfers between devices, on_device(): up = lax.ppermute(bottom, 'rows', ahead)  4.87 us
    all_to_all x1, waiting for transfers between devices, on_device(): first = lax.all_to_all(slots, ('rows', 'cols'), 0, 0, tiled=True)  4.03 us
    ppermute x1, starting transfers between devices, on_device(): left = lax.ppermute(strip[:, TILE_C - LANES:], 'cols', ahead)  3.03 us
  transfers between devices with their start and end apart: 5, of which 1 were waited for; matrix products, arithmetic and copies ran while one was open for 0% of the time, Pallas kernels for 25%

profile of v3, /device:TPU:0, one launch (start us, length us, event | category | flops | bytes accessed | tf_op | source)
XLA Modules:
  0.0 74.1 jit_solution(12314693873298263155)
XLA Ops:
  0.6 0.0 copy-start.1
  0.6 0.0 copy-start.2
  0.7 0.0 copy-start.3
  0.7 10.9 %density.1 = (f32[64,512]{1,0:T(8,128)}, f32[8,512]{1,0:T(8,128)}, f32[8,512]{1,0:T(8,128)}, f32[256,128]{1,0:T(8,128)}, f32[256,128]{1,0:T(8,128)}) custom-call(s32[256,128]{1,0:T(8,128)} %bitcast.4, bf16[256,128]{1,0:T(8,128)(2,1)} %bitcast.8, s32[4,16384]{1,0:T(4,128)} %box_ref.1, s32[256,128]{1,0:T(8,128)} %bitcast.6), custom_call_target="tpu_custom_call" | custom-call | tf_op jit(solution)/shard_map/density/pallas_call | solution.py:378
  11.6 4.9 %collective-permute-start = (f32[8,512]{1,0:T(8,128)}, f32[8,512]{1,0:T(8,128)S(1)}, u32[]{:S(2)}, u32[]{:S(2)}) collective-permute-start(f32[8,512]{1,0:T(8,128)} %get-tuple-element.22), channel_id=1, source_target_pairs={{0,4},{4,8},{8,12},{12,16},{16,20},{20,24},{24,28},{1,5},{5,9},{9,... | collective-permute-start | bytes 49160 | tf_op jit(solution)/shard_map/ppermute | solution.py:386
  16.5 1.3 %collective-permute-start.1 = (f32[8,512]{1,0:T(8,128)}, f32[8,512]{1,0:T(8,128)S(1)}, u32[]{:S(2)}, u32[]{:S(2)}) collective-permute-start(f32[8,512]{1,0:T(8,128)} %get-tuple-element.23), channel_id=1, source_target_pairs={{4,0},{8,4},{12,8},{16,12},{20,16},{24,20},{28,24},{5,1},{9,5},{13... | collective-permute-start | bytes 49160 | tf_op jit(solution)/shard_map/ppermute | solution.py:387
  17.8 0.0 copy-done.1
  17.8 0.0 copy-done.2
  17.8 0.0 copy-done.3
  17.8 0.0 copy-start.4
  17.8 0.9 %copy-done.4 = f32[256,128]{1,0:T(8,128)S(1)} copy-done((f32[256,128]{1,0:T(8,128)S(1)}, f32[256,128]{1,0:T(8,128)}, u32[]{:S(2)}) %copy-start.4) | copy-done | bytes 131096
  18.7 0.0 copy-start.5
  18.7 0.9 %copy-done.5 = f32[256,128]{1,0:T(8,128)S(1)} copy-done((f32[256,128]{1,0:T(8,128)S(1)}, f32[256,128]{1,0:T(8,128)}, u32[]{:S(2)}) %copy-start.5) | copy-done | bytes 131096
  19.6 0.0 copy-start
  19.6 7.1 %order.1 = (f32[32,2,16,128]{3,2,1,0:T(8,128)}, s32[256,128]{1,0:T(8,128)S(1)}, s32[8,128]{1,0:T(8,128)S(1)}) custom-call(s32[256,128]{1,0:T(8,128)S(1)} %bitcast.5, bf16[256,128]{1,0:T(8,128)(2,1)S(1)} %bitcast.9, s32[256,128]{1,0:T(8,128)S(1)} %bitcast.7, f32[256,128]{1,0:T(8,128)S(1)} %copy-done.4, f32[256,128]{1,0:T(8,128)S(1)} %copy-done.5), custom_call_target="tpu_custom_call" | custom-call | flops 15000000512 | bytes 2000000 | tf_op jit(solution)/shard_map/order/pallas_call | solution.py:388
  26.7 0.0 collective-permute-done.up_ref
  26.7 0.0 collective-permute-done.1.down_ref
  26.8 0.0 copy-done
  26.8 1.3 %collective-permute-start.3 = (f32[80,128]{1,0:T(8,128)S(1)}, f32[80,128]{1,0:T(8,128)S(1)}, u32[]{:S(2)}, u32[]{:S(2)}) collective-permute-start(f32[80,128]{1,0:T(8,128)S(1)} %get-tuple-element.33), channel_id=1, source_target_pairs={{1,0},{2,1},{3,2},{5,4},{6,5},{7,6},{9,8},{10,9},{11,10},{13,12},{... | collective-permute-start | bytes 122888 | tf_op jit(solution)/shard_map/ppermute | solution.py:402
  28.1 3.0 %collective-permute-start.2 = (f32[80,128]{1,0:T(8,128)S(1)}, f32[80,128]{1,0:T(8,128)S(1)}, u32[]{:S(2)}, u32[]{:S(2)}) collective-permute-start(f32[80,128]{1,0:T(8,128)S(1)} %get-tuple-element.34), channel_id=1, source_target_pairs={{0,1},{1,2},{2,3},{4,5},{5,6},{6,7},{8,9},{9,10},{10,11},{12,13},{... | collective-permute-start | bytes 122888 | tf_op jit(solution)/shard_map/ppermute | solution.py:401
  31.2 7.0 %all-to-all-start = ((f32[32,2,16,128]{3,2,1,0:T(8,128)}), f32[32,2,16,128]{3,2,1,0:T(8,128)S(1)}, u32[]{:S(2)}, u32[]{:S(2)}) async-start(f32[32,2,16,128]{3,2,1,0:T(8,128)} %get-tuple-element.29), calls=%async_computation | async-start | bytes 1048576 | tf_op jit(solution)/shard_map/all_to_all | solution.py:403
  38.2 0.0 collective-permute-done.3.right_ref
  38.2 0.0 collective-permute-done.2.left_ref
  38.2 11.6 %flow.1 = (f32[64,512]{1,0:T(8,128)}, f32[32,2,16,128]{3,2,1,0:T(8,128)S(1)}) custom-call(s32[8,128]{1,0:T(8,128)S(1)} %get-tuple-element.20.starts_ref, f32[64,512]{1,0:T(8,128)S(1)} %copy-done, f32[8,512]{1,0:T(8,128)S(1)} %collective-permute-done.up_ref, f32[8,512]{1,0:T(8,128)S(1)} %collective-permute-done.1.down_ref, ...), custom_call_target="tpu_custom_call" | custom-call | flops 15000000512 | bytes 2000000 | tf_op jit(solution)/shard_map/flow/pallas_call | solution.py:405
  49.8 4.0 %all-to-all-done.first_ref = f32[32,2,16,128]{3,2,1,0:T(8,128)S(1)} async-done(((f32[32,2,16,128]{3,2,1,0:T(8,128)}), f32[32,2,16,128]{3,2,1,0:T(8,128)S(1)}, u32[]{:S(2)}, u32[]{:S(2)}) %all-to-all-start) | async-done | bytes 524320 | tf_op jit(solution)/shard_map/all_to_all | solution.py:403
  53.8 18.4 %all_to_all.10.second_ref = f32[32,2,16,128]{3,2,1,0:T(8,128)S(1)} all-to-all(f32[32,2,16,128]{3,2,1,0:T(8,128)S(1)} %get-tuple-element.30), channel_id=1, replica_groups=mesh['rows'=8,'cols'=4] {'rows','cols'}, dimensions={0} | all-to-all | bytes 1048576 | tf_op jit(solution)/shard_map/all_to_all | solution.py:414
  72.2 1.9 %merge.1 = (f32[3,65536]{1,0:T(4,128)}, s32[512,128]{1,0:T(8,128)}) custom-call(f32[32,2,16,128]{3,2,1,0:T(8,128)S(1)} %all-to-all-done.first_ref, f32[32,2,16,128]{3,2,1,0:T(8,128)S(1)} %all_to_all.10.second_ref), custom_call_target="tpu_custom_call" | custom-call | tf_op jit(solution)/shard_map/merge/pallas_call | solution.py:418
  (4 shorter events, 0.0 us)
Async XLA Ops:
  0.6 17.1 %copy-start.1 = (s32[32768]{0:T(1024)S(1)}, s32[32768]{0:T(1024)}, u32[]{:S(2)}) copy-start(s32[32768]{0:T(1024)} %param.4) | copy-start | bytes 393220
  0.6 17.1 %copy-start.2 = (s32[32768]{0:T(1024)S(1)}, s32[32768]{0:T(1024)}, u32[]{:S(2)}) copy-start(s32[32768]{0:T(1024)} %param.6) | copy-start | bytes 393220
  0.7 17.1 %copy-start.3 = (bf16[32768]{0:T(1024)(128)(2,1)S(1)}, bf16[32768]{0:T(1024)(128)(2,1)}, u32[]{:S(2)}) copy-start(bf16[32768]{0:T(1024)(128)(2,1)} %param.5) | copy-start | bytes 196612
  11.6 15.1 %collective-permute-start = (f32[8,512]{1,0:T(8,128)}, f32[8,512]{1,0:T(8,128)S(1)}, u32[]{:S(2)}, u32[]{:S(2)}) collective-permute-start(f32[8,512]{1,0:T(8,128)} %get-tuple-element.22), channel_id=1, source_target_pairs={{0,4},{4,8},{8,12},{12,16},{16,20},{20,24},{24,28},{1,5},{5,9},{9,... | collective-permute-start | bytes 49160 | tf_op jit(solution)/shard_map/ppermute | solution.py:386
  16.5 10.3 %collective-permute-start.1 = (f32[8,512]{1,0:T(8,128)}, f32[8,512]{1,0:T(8,128)S(1)}, u32[]{:S(2)}, u32[]{:S(2)}) collective-permute-start(f32[8,512]{1,0:T(8,128)} %get-tuple-element.23), channel_id=1, source_target_pairs={{4,0},{8,4},{12,8},{16,12},{20,16},{24,20},{28,24},{5,1},{9,5},{13... | collective-permute-start | bytes 49160 | tf_op jit(solution)/shard_map/ppermute | solution.py:387
  17.8 0.9 %copy-start.4 = (f32[256,128]{1,0:T(8,128)S(1)}, f32[256,128]{1,0:T(8,128)}, u32[]{:S(2)}) copy-start(f32[256,128]{1,0:T(8,128)} %get-tuple-element.18.pre_ref) | copy-start | bytes 393220
  18.7 0.9 %copy-start.5 = (f32[256,128]{1,0:T(8,128)S(1)}, f32[256,128]{1,0:T(8,128)}, u32[]{:S(2)}) copy-start(f32[256,128]{1,0:T(8,128)} %get-tuple-element.19.cnt_ref) | copy-start | bytes 393220
  19.6 7.2 %copy-start = (f32[64,512]{1,0:T(8,128)S(1)}, f32[64,512]{1,0:T(8,128)}, u32[]{:S(2)}) copy-start(f32[64,512]{1,0:T(8,128)} %get-tuple-element.21.dens_in) | copy-start | bytes 393220
  26.8 11.4 %collective-permute-start.3 = (f32[80,128]{1,0:T(8,128)S(1)}, f32[80,128]{1,0:T(8,128)S(1)}, u32[]{:S(2)}, u32[]{:S(2)}) collective-permute-start(f32[80,128]{1,0:T(8,128)S(1)} %get-tuple-element.33), channel_id=1, source_target_pairs={{1,0},{2,1},{3,2},{5,4},{6,5},{7,6},{9,8},{10,9},{11,10},{13,12},{... | collective-permute-start | bytes 122888 | tf_op jit(solution)/shard_map/ppermute | solution.py:402
  28.1 10.1 %collective-permute-start.2 = (f32[80,128]{1,0:T(8,128)S(1)}, f32[80,128]{1,0:T(8,128)S(1)}, u32[]{:S(2)}, u32[]{:S(2)}) collective-permute-start(f32[80,128]{1,0:T(8,128)S(1)} %get-tuple-element.34), channel_id=1, source_target_pairs={{0,1},{1,2},{2,3},{4,5},{5,6},{6,7},{8,9},{9,10},{10,11},{12,13},{... | collective-permute-start | bytes 122888 | tf_op jit(solution)/shard_map/ppermute | solution.py:401
  31.2 22.6 %all-to-all-start = ((f32[32,2,16,128]{3,2,1,0:T(8,128)}), f32[32,2,16,128]{3,2,1,0:T(8,128)S(1)}, u32[]{:S(2)}, u32[]{:S(2)}) async-start(f32[32,2,16,128]{3,2,1,0:T(8,128)} %get-tuple-element.29), calls=%async_computation | async-start | bytes 1048576 | tf_op jit(solution)/shard_map/all_to_all | solution.py:403

commit v4 on v3

--- a/solution.py
+++ b/solution.py
@@ -14,12 +14,13 @@
 LANES = 128
 EDGE = 8
 DIRECT = 8
-BY_DOT = 12
+BY_DOT = 16
 BF16 = jnp.bfloat16
 F8 = jnp.float8_e4m3fn
 SMALL = 64.0
 SYMBOLS = 119
 GRANT = 24 * 2 ** 20
+FULL = 62 * 2 ** 20
 BASE = 233
 F32 = jnp.float32
 
@@ -105,19 +106,29 @@
     )
 
 
+def same(iota, row):
+    rows, lanes = iota.shape
+    packed = jnp.broadcast_to(row, (32, lanes)).astype(jnp.int8)
+    return iota == jnp.broadcast_to(packed[None], (rows // 32, 32, lanes)).reshape(rows, lanes)
+
+
+def spread8(row, rows):
+    lanes = row.shape[1]
+    packed = jnp.broadcast_to(row, (32, lanes)).astype(F8)
+    return jnp.broadcast_to(packed[None], (rows // 32, 32, lanes)).reshape(rows, lanes)
+
+
 def placed(refs, s_ref, w_ref, first, group):
-    nil = jnp.zeros((), BF16)
-    one = jnp.ones((), BF16)
-    s_iota = narrow(sublane_iota(LANES))
-    w_iota = narrow(sublane_iota(2 * LANES))
+    nil = jnp.zeros((), F8)
+    one = jnp.ones((), F8)
+    s_iota = sublane_iota(LANES).astype(jnp.int8)
+    w_iota = (sublane_iota(2 * LANES) - LANES).astype(jnp.int8)
     left, right = [], []
     for j in range(group):
         here = pl.ds(first + j, 1)
-        hit = s_iota == spread(s_ref[here, :], LANES)
-        left.append(
-            jnp.concatenate([jnp.where(hit, spread(x[here, :], LANES), nil).astype(F8) for x in refs], axis=0)
-        )
-        right.append(jnp.where(w_iota == spread(w_ref[here, :], 2 * LANES), one, nil).astype(F8))
+        hit = same(s_iota, s_ref[here, :])
+        left.append(jnp.concatenate([jnp.where(hit, spread8(x[here, :], LANES), nil) for x in refs], axis=0))
+        right.append(jnp.where(same(w_iota, w_ref[here, :]), one, nil))
     return dot_nt(jnp.concatenate(left, axis=1), jnp.concatenate(right, axis=1))
 
 
@@ -128,16 +139,24 @@
     return narrow(sublane_iota(LANES, lanes) < lax.broadcasted_iota(jnp.int32, (LANES, lanes), 1))
 
 
-def density_kernel(parts, bin_ref, area_ref, box_ref, owner_ref, dens_ref, top_ref, bottom_ref, pre_ref, cnt_ref,
-                   s_ref, w_ref, a_ref, b_ref, raw_ref, cong_ref):
+def density_kernel(parts, bin_hbm, area_hbm, box_hbm, owner_hbm, dens_ref, top_ref, bottom_ref, starts_ref, s_ref, w_ref,
+                   a_ref, b_ref, bin_ref, area_ref, box_ref, owner_ref, pre_ref, cnt_ref, raw_ref, cong_ref, sem):
+    pairs = ((bin_hbm, bin_ref), (area_hbm, area_ref), (box_hbm, box_ref), (owner_hbm, owner_ref))
+    copies = [pltpu.make_async_copy(x, y, sem.at[k]) for k, (x, y) in enumerate(pairs)]
+    for copy in copies:
+        copy.start()
+    raw_ref[...] = jnp.zeros_like(raw_ref)
+    cong_ref[...] = jnp.zeros_like(cong_ref)
+    copies[0].wait()
+    copies[1].wait()
     all_rows = bin_ref.shape[0]
     bins = bin_ref[...]
     area = area_ref[...].astype(F32)
-    s_ref[...] = (((bins >> 8) & 1) * TILE_R + (bins >> 9)).astype(F32)
-    w_ref[...] = (bins & 255).astype(F32)
+    s_ref[...] = ((bins >> 8) & 1) * TILE_R + (bins >> 9)
+    w_ref[...] = (bins & 255) - LANES
     a_ref[...], b_ref[...] = halves(area)
-    raw_ref[...] = jnp.zeros_like(raw_ref)
-    cong_ref[...] = jnp.zeros_like(cong_ref)
+    copies[2].wait()
+    copies[3].wait()
     nil = jnp.zeros((), BF16)
     one = jnp.ones((), BF16)
     steps = STEPS
@@ -145,7 +164,9 @@
     width = box_ref.shape[1] // steps
     r_iota = narrow(sublane_iota(TILE_R, width))
     c_iota = narrow(sublane_iota(TILE_C, width) - TILE_C // 2)
-    upper = before(2 * LANES)
+    upper = before(2 * LANES).astype(F8)
+    nil8 = jnp.zeros((), F8)
+    one8 = jnp.ones((), F8)
     lane = lax.broadcasted_iota(jnp.int32, (group, LANES), 1)
     many = 8
 
@@ -167,11 +188,13 @@
         )
         here = pl.ds(pl.multiple_of(k * group, group), group)
         owner = owner_ref[here, :]
+        owner8 = owner.astype(jnp.int8)
         prefix = jnp.zeros((group, LANES), F32)
         counts = jnp.zeros((group, LANES), F32)
         for g in range(0, parts, many):
             hits = [owner == g + m for m in range(many)]
-            sums = jnp.dot(jnp.concatenate([narrow(h) for h in hits], axis=0), upper, preferred_element_type=F32)
+            masks = [jnp.where(owner8 == jnp.int8(g + m), one8, nil8) for m in range(many)]
+            sums = jnp.dot(jnp.concatenate(masks, axis=0), upper, preferred_element_type=F32)
             for m in range(many):
                 part = sums[m * group : (m + 1) * group]
                 prefix = jnp.where(hits[m], part[:, :LANES], prefix)
@@ -190,11 +213,6 @@
     top_ref[...] = dens[:EDGE]
     bottom_ref[...] = dens[TILE_R - EDGE :]
 
-
-def order_kernel(parts, bin_ref, area_ref, owner_ref, pre_ref, cnt_ref, slots_ref, sorted_ref, starts_ref,
-                 s_ref, w_ref, a_ref, b_ref, c_ref, acc_ref, run_bin_ref, run_area_ref, vec_ref, smem_ref, sem):
-    all_rows = bin_ref.shape[0]
-    group = all_rows // STEPS
     counts = cnt_ref[...]
     lower = narrow(
         lax.broadcasted_iota(jnp.int32, (all_rows, all_rows), 1)
@@ -209,25 +227,35 @@
         high.astype(BF16), strict, preferred_element_type=F32
     )
     starts = jnp.broadcast_to(first[7:8], (8, LANES))
-    vec_ref[...] = starts.astype(jnp.int32)
     starts_ref[...] = starts.astype(jnp.int32)
-    copy = pltpu.make_async_copy(vec_ref, smem_ref, sem)
-    copy.start()
     dest = (pre_ref[...] + jnp.take_along_axis(base + starts[:1], owner_ref[...], axis=1)).astype(jnp.int32)
     half = all_rows // 2
     top = jnp.where(dest >= half * LANES, 1, 0)
-    s_ref[...] = ((dest >> 7) - top * half).astype(F32)
-    w_ref[...] = ((dest & (LANES - 1)) + top * LANES).astype(F32)
-    rest, digit = divide(area_code(area_ref[...].astype(F32)) * (TILE_R * TILE_C) + bin_ref[...], BASE)
-    c_ref[...] = symbol(digit)
-    rest, digit = divide(rest, BASE)
-    b_ref[...] = symbol(digit)
-    a_ref[...] = symbol(rest)
+    s_ref[...] = (dest >> 7) - top * half
+    w_ref[...] = (dest & (LANES - 1)) + top * LANES - LANES
+
+
+def order_kernel(parts, starts_ref, s_ref, w_ref, bin_ref, area_ref, slots_ref, sorted_ref, a_ref, b_ref, c_ref, acc_ref, run_bin_ref, run_area_ref):
+    all_rows = s_ref.shape[0]
+    half = all_rows // 2
+    group = all_rows // STEPS
     acc_ref[...] = jnp.zeros_like(acc_ref)
+
+    def encode(k):
+        here = pl.ds(pl.multiple_of(k * group, group), group)
+        code = area_code(area_ref[here, :].astype(F32)) * (TILE_R * TILE_C) + bin_ref[here, :]
+        rest, last = divide(code, BASE)
+        first, middle = divide(rest, BASE)
+        a_ref[here, :] = symbol(first)
+        b_ref[here, :] = symbol(middle)
+        c_ref[here, :] = symbol(last)
 
     def place(k, carry):
         acc_ref[...] += placed((a_ref, b_ref, c_ref), s_ref, w_ref, k * group, group)
+        encode(lax.rem(k + 1, STEPS))
         return carry
+
+    encode(0)
 
     lax.fori_loop(0, STEPS, place, 0)
     for h in range(2):
@@ -243,8 +271,7 @@
     pad = slice(all_rows, run_bin_ref.shape[0])
     run_bin_ref[pad, :] = jnp.zeros((run_bin_ref.shape[0] - all_rows, LANES), F32)
     run_area_ref[pad, :] = jnp.zeros((run_bin_ref.shape[0] - all_rows, LANES), F32)
-    copy.wait()
-    expand(parts, smem_ref, all_rows * LANES, ((run_bin_ref, 0, slots_ref, -1.0), (run_area_ref, 1, slots_ref, 0.0)))
+    expand(parts, starts_ref, all_rows * LANES, ((run_bin_ref, 0, slots_ref, -1.0), (run_area_ref, 1, slots_ref, 0.0)))
 
 
 def flow_kernel(parts, grid_rows, grid_cols, starts_ref, dens_in, up_ref, down_ref, left_ref, right_ref, sorted_ref,
@@ -375,25 +402,32 @@
     runs = vmem(rows + spare, LANES)
     table = shape(rows, LANES)
     grant = pltpu.CompilerParams(vmem_limit_bytes=GRANT)
-    dens, top, bottom, prefix, counts = pl.pallas_call(
+    whole_ints = shape(rows, LANES, dtype=jnp.int32)
+    int_cells = vmem(rows, LANES, dtype=jnp.int32)
+    dens, top, bottom, starts, s, w = pl.pallas_call(
         functools.partial(density_kernel, parts),
-        out_shape=(shape(TILE_R, TILE_C), shape(EDGE, TILE_C), shape(EDGE, TILE_C), table, table),
-        scratch_shapes=[cells] * 4 + [vmem(2 * LANES, 2 * LANES), vmem(TILE_C, 2 * TILE_R)],
+        out_shape=(shape(TILE_R, TILE_C), shape(EDGE, TILE_C), shape(EDGE, TILE_C), shape(8, LANES, dtype=jnp.int32),
+                   whole_ints, whole_ints),
+        in_specs=[pl.BlockSpec(memory_space=pltpu.HBM)] * 4,
+        scratch_shapes=[cells, cells, int_cells, vmem(rows, LANES, dtype=BF16), vmem(*net_box.shape, dtype=jnp.int32), int_cells, cells, cells,
+                        vmem(2 * LANES, 2 * LANES), vmem(TILE_C, 2 * TILE_R), pltpu.SemaphoreType.DMA((4,))],
+        compiler_params=pltpu.CompilerParams(vmem_limit_bytes=FULL),
         name="density",
     )(bins, area, net_box, owner)
     ahead = [(k, k + 1) for k in range(n_rows - 1)]
     behind = [(k + 1, k) for k in range(n_rows - 1)]
     up = lax.ppermute(bottom, "rows", ahead)
     down = lax.ppermute(top, "rows", behind)
-    slots, in_order, starts = pl.pallas_call(
+    scalars = pl.BlockSpec(memory_space=pltpu.SMEM)
+    slots, in_order = pl.pallas_call(
         functools.partial(order_kernel, parts),
-        out_shape=(shape(parts, 2, per, LANES), shape(rows, LANES, dtype=jnp.int32), shape(8, LANES, dtype=jnp.int32)),
-        scratch_shapes=[cells] * 5 + [vmem(3 * LANES, 2 * LANES), runs, runs]
-        + [vmem(8, LANES, dtype=jnp.int32), pltpu.SMEM((8, LANES), jnp.int32), pltpu.SemaphoreType.DMA],
-        compiler_params=grant,
+        out_shape=(shape(parts, 2, per, LANES), whole_ints),
+        in_specs=[scalars] + [pl.BlockSpec()] * 4,
+        scratch_shapes=[cells, cells, cells, vmem(3 * LANES, 2 * LANES), runs, runs],
+        compiler_params=pltpu.CompilerParams(vmem_limit_bytes=FULL),
         cost_estimate=pl.CostEstimate(flops=15_000_000_000, bytes_accessed=2_000_000, transcendentals=0),
         name="order",
-    )(bins, area, owner, prefix, counts)
+    )(starts, s, w, bins, area)
     up, down, slots = lax.optimization_barrier((up, down, slots))
     strip = jnp.concatenate([up, dens, down], axis=0)
     ahead = [(k, k + 1) for k in range(n_cols - 1)]
@@ -401,7 +435,6 @@
     left = lax.ppermute(strip[:, TILE_C - LANES :], "cols", ahead)
     right = lax.ppermute(strip[:, :LANES], "cols", behind)
     first = lax.all_to_all(slots, ("rows", "cols"), 0, 0, tiled=True)
-    scalars = pl.BlockSpec(memory_space=pltpu.SMEM)
     density, shifts = pl.pallas_call(
         functools.partial(flow_kernel, parts, grid_rows, grid_cols),
         out_shape=(shape(TILE_R, TILE_C), shape(parts, 2, per, LANES)),

time: 74.4 us -> 71.1 us (0.956)
  Pallas kernels: 31.5 us -> 29.3 us
  local copies, waits for them, and re-layouts: 1.85 us -> 0.04 us
    unnamed x14 -> x8, local copies, waits for them, and re-layouts: 1.83 us -> 0.03 us
    pallas_call x1, Pallas kernels: 10.9 us -> 9.17 us  [on_device(): pl.pallas_call(functools.partial(density_kernel, parts), out_shape=(shape...]
  transfers between devices with their start and end apart: 5 -> 5, of which waited for: 1 -> 1; matrix products, arithmetic and copies ran while one was open for 0% -> 0% of each run, Pallas kernels for 25% -> 26%
where the time goes in v4:
time: 71.1 us; the launch traced here: 70.7 us
  Pallas kernels  29.3 us (41%)
  blocking collectives  18.4 us (26%)
  starting transfers between devices  17.6 us (25%)
  waiting for transfers between devices  4.6 us (6%)
  between operations  0.78 us (1%)
    all_to_all x1, blocking collectives, on_device(): second = lax.all_to_all(shifts, ('rows', 'cols'), 0, 0, tiled=True)  18.4 us
    pallas_call x1, Pallas kernels, on_device(): pl.pallas_call(functools.partial(flow_kernel, parts, grid_rows, grid_cols...  11 us
    pallas_call x1, Pallas kernels, on_device(): pl.pallas_call(functools.partial(density_kernel, parts), out_shape=(shape...  9.17 us
    pallas_call x1, Pallas kernels, on_device(): pl.pallas_call(functools.partial(order_kernel, parts), out_shape=(shape(p...  7.28 us
    all_to_all x1, starting transfers between devices, on_device(): first = lax.all_to_all(slots, ('rows', 'cols'), 0, 0, tiled=True)  7.01 us
    ppermute x1, starting transfers between devices, on_device(): up = lax.ppermute(bottom, 'rows', ahead)  4.87 us
    all_to_all x1, waiting for transfers between devices, on_device(): first = lax.all_to_all(slots, ('rows', 'cols'), 0, 0, tiled=True)  4.59 us
    ppermute x1, starting transfers between devices, on_device(): left = lax.ppermute(strip[:, TILE_C - LANES:], 'cols', ahead)  3.16 us
  transfers between devices with their start and end apart: 5, of which 1 were waited for; matrix products, arithmetic and copies ran while one was open for 0% of the time, Pallas kernels for 26%

profile of v4, /device:TPU:0, one launch (start us, length us, event | category | flops | bytes accessed | tf_op | source)
XLA Modules:
  0.0 70.7 jit_solution(4155185444412635582)
XLA Ops:
  0.6 9.2 %density.1 = (f32[64,512]{1,0:T(8,128)}, f32[8,512]{1,0:T(8,128)}, f32[8,512]{1,0:T(8,128)}, s32[8,128]{1,0:T(8,128)}, s32[256,128]{1,0:T(8,128)}, /*index=5*/s32[256,128]{1,0:T(8,128)}) custom-call(s32[256,128]{1,0:T(8,128)} %bitcast.5, bf16[256,128]{1,0:T(8,128)(2,1)} %bitcast.7, s32[4,16384]{1,0:T(4,128)} %box_hbm.1, s32[256,128]{1,0:T(8,128)} %bitcast.4), custom_call_target="tpu_custom_call" | custom-call | tf_op jit(solution)/shard_map/density/pallas_call | solution.py:407
  9.8 4.9 %collective-permute-start = (f32[8,512]{1,0:T(8,128)}, f32[8,512]{1,0:T(8,128)S(1)}, u32[]{:S(2)}, u32[]{:S(2)}) collective-permute-start(f32[8,512]{1,0:T(8,128)} %get-tuple-element.20), channel_id=1, source_target_pairs={{0,4},{4,8},{8,12},{12,16},{16,20},{20,24},{24,28},{1,5},{5,9},{9,... | collective-permute-start | bytes 49160 | tf_op jit(solution)/shard_map/ppermute | solution.py:419
  14.7 1.3 %collective-permute-start.1 = (f32[8,512]{1,0:T(8,128)}, f32[8,512]{1,0:T(8,128)S(1)}, u32[]{:S(2)}, u32[]{:S(2)}) collective-permute-start(f32[8,512]{1,0:T(8,128)} %get-tuple-element.21), channel_id=1, source_target_pairs={{4,0},{8,4},{12,8},{16,12},{20,16},{24,20},{28,24},{5,1},{9,5},{13... | collective-permute-start | bytes 49160 | tf_op jit(solution)/shard_map/ppermute | solution.py:420
  16.0 0.0 copy-start
  16.0 7.3 %order.1 = (f32[32,2,16,128]{3,2,1,0:T(8,128)}, s32[256,128]{1,0:T(8,128)}) custom-call(s32[8,128]{1,0:T(8,128)} %get-tuple-element.18.starts_ref, s32[256,128]{1,0:T(8,128)} %get-tuple-element.22.s_ref, s32[256,128]{1,0:T(8,128)} %get-tuple-element.23.w_ref, s32[256,128]{1,0:T(8,128)} %bitcast.6, bf16[256,128]{1,0:T(8,128)(2,1)} %bitcast.8), custom_call_target="tpu_custom_call" | custom-call | flops 15000000512 | bytes 2000000 | tf_op jit(solution)/shard_map/order/pallas_call | solution.py:422
  23.3 0.0 collective-permute-done.up_ref
  23.3 0.0 collective-permute-done.1.down_ref
  23.3 0.0 copy-done
  23.4 1.3 %collective-permute-start.3 = (f32[80,128]{1,0:T(8,128)S(1)}, f32[80,128]{1,0:T(8,128)S(1)}, u32[]{:S(2)}, u32[]{:S(2)}) collective-permute-start(f32[80,128]{1,0:T(8,128)S(1)} %get-tuple-element.33), channel_id=1, source_target_pairs={{1,0},{2,1},{3,2},{5,4},{6,5},{7,6},{9,8},{10,9},{11,10},{13,12},{... | collective-permute-start | bytes 122888 | tf_op jit(solution)/shard_map/ppermute | solution.py:436
  24.7 0.0 copy-start.1
  24.7 0.0 copy-start.2
  24.7 3.2 %collective-permute-start.2 = (f32[80,128]{1,0:T(8,128)S(1)}, f32[80,128]{1,0:T(8,128)S(1)}, u32[]{:S(2)}, u32[]{:S(2)}) collective-permute-start(f32[80,128]{1,0:T(8,128)S(1)} %get-tuple-element.34), channel_id=1, source_target_pairs={{0,1},{1,2},{2,3},{4,5},{5,6},{6,7},{8,9},{9,10},{10,11},{12,13},{... | collective-permute-start | bytes 122888 | tf_op jit(solution)/shard_map/ppermute | solution.py:435
  27.9 7.0 %all-to-all-start = ((f32[32,2,16,128]{3,2,1,0:T(8,128)}), f32[32,2,16,128]{3,2,1,0:T(8,128)S(1)}, u32[]{:S(2)}, u32[]{:S(2)}) async-start(f32[32,2,16,128]{3,2,1,0:T(8,128)} %get-tuple-element.29), calls=%async_computation | async-start | bytes 1048576 | tf_op jit(solution)/shard_map/all_to_all | solution.py:437
  34.9 0.0 collective-permute-done.3.right_ref
  34.9 0.0 collective-permute-done.2.left_ref
  34.9 0.0 copy-done.1
  34.9 0.0 copy-done.2
  34.9 11.0 %flow.1 = (f32[64,512]{1,0:T(8,128)}, f32[32,2,16,128]{3,2,1,0:T(8,128)S(1)}) custom-call(s32[8,128]{1,0:T(8,128)S(1)} %copy-done.1, f32[64,512]{1,0:T(8,128)S(1)} %copy-done, f32[8,512]{1,0:T(8,128)S(1)} %collective-permute-done.up_ref, f32[8,512]{1,0:T(8,128)S(1)} %collective-permute-done.1.down_ref, f32[80,128]{1,0:T(8,128)S(1)} %collective-permute-done.2.left_ref, ...), custom_call_target="tpu_custom_call" | custom-call | flops 15000000512 | bytes 2000000 | tf_op jit(solution)/shard_map/flow/pallas_call | solution.py:438
  45.9 4.6 %all-to-all-done.first_ref = f32[32,2,16,128]{3,2,1,0:T(8,128)S(1)} async-done(((f32[32,2,16,128]{3,2,1,0:T(8,128)}), f32[32,2,16,128]{3,2,1,0:T(8,128)S(1)}, u32[]{:S(2)}, u32[]{:S(2)}) %all-to-all-start) | async-done | bytes 524320 | tf_op jit(solution)/shard_map/all_to_all | solution.py:437
  50.5 18.4 %all_to_all.10.second_ref = f32[32,2,16,128]{3,2,1,0:T(8,128)S(1)} all-to-all(f32[32,2,16,128]{3,2,1,0:T(8,128)S(1)} %get-tuple-element.30), channel_id=1, replica_groups=mesh['rows'=8,'cols'=4] {'rows','cols'}, dimensions={0} | all-to-all | bytes 1048576 | tf_op jit(solution)/shard_map/all_to_all | solution.py:447
  68.9 1.9 %merge.1 = (f32[3,65536]{1,0:T(4,128)}, s32[512,128]{1,0:T(8,128)}) custom-call(f32[32,2,16,128]{3,2,1,0:T(8,128)S(1)} %all-to-all-done.first_ref, f32[32,2,16,128]{3,2,1,0:T(8,128)S(1)} %all_to_all.10.second_ref), custom_call_target="tpu_custom_call" | custom-call | tf_op jit(solution)/shard_map/merge/pallas_call | solution.py:451
  (4 shorter events, 0.0 us)
Async XLA Ops:
  9.8 13.5 %collective-permute-start = (f32[8,512]{1,0:T(8,128)}, f32[8,512]{1,0:T(8,128)S(1)}, u32[]{:S(2)}, u32[]{:S(2)}) collective-permute-start(f32[8,512]{1,0:T(8,128)} %get-tuple-element.20), channel_id=1, source_target_pairs={{0,4},{4,8},{8,12},{12,16},{16,20},{20,24},{24,28},{1,5},{5,9},{9,... | collective-permute-start | bytes 49160 | tf_op jit(solution)/shard_map/ppermute | solution.py:419
  14.7 8.6 %collective-permute-start.1 = (f32[8,512]{1,0:T(8,128)}, f32[8,512]{1,0:T(8,128)S(1)}, u32[]{:S(2)}, u32[]{:S(2)}) collective-permute-start(f32[8,512]{1,0:T(8,128)} %get-tuple-element.21), channel_id=1, source_target_pairs={{4,0},{8,4},{12,8},{16,12},{20,16},{24,20},{28,24},{5,1},{9,5},{13... | collective-permute-start | bytes 49160 | tf_op jit(solution)/shard_map/ppermute | solution.py:420
  16.0 7.3 %copy-start = (f32[64,512]{1,0:T(8,128)S(1)}, f32[64,512]{1,0:T(8,128)}, u32[]{:S(2)}) copy-start(f32[64,512]{1,0:T(8,128)} %get-tuple-element.19.dens_in) | copy-start | bytes 393220
  23.4 11.5 %collective-permute-start.3 = (f32[80,128]{1,0:T(8,128)S(1)}, f32[80,128]{1,0:T(8,128)S(1)}, u32[]{:S(2)}, u32[]{:S(2)}) collective-permute-start(f32[80,128]{1,0:T(8,128)S(1)} %get-tuple-element.33), channel_id=1, source_target_pairs={{1,0},{2,1},{3,2},{5,4},{6,5},{7,6},{9,8},{10,9},{11,10},{13,12},{... | collective-permute-start | bytes 122888 | tf_op jit(solution)/shard_map/ppermute | solution.py:436
  24.7 10.2 %copy-start.1 = (s32[8,128]{1,0:T(8,128)S(1)}, s32[8,128]{1,0:T(8,128)}, u32[]{:S(2)}) copy-start(s32[8,128]{1,0:T(8,128)} %get-tuple-element.18.starts_ref) | copy-start | bytes 12292
  24.7 10.2 %copy-start.2 = (s32[256,128]{1,0:T(8,128)S(1)}, s32[256,128]{1,0:T(8,128)}, u32[]{:S(2)}) copy-start(s32[256,128]{1,0:T(8,128)} %get-tuple-element.27.sorted_ref) | copy-start | bytes 393220
  24.7 10.2 %collective-permute-start.2 = (f32[80,128]{1,0:T(8,128)S(1)}, f32[80,128]{1,0:T(8,128)S(1)}, u32[]{:S(2)}, u32[]{:S(2)}) collective-permute-start(f32[80,128]{1,0:T(8,128)S(1)} %get-tuple-element.34), channel_id=1, source_target_pairs={{0,1},{1,2},{2,3},{4,5},{5,6},{6,7},{8,9},{9,10},{10,11},{12,13},{... | collective-permute-start | bytes 122888 | tf_op jit(solution)/shard_map/ppermute | solution.py:435
  27.9 22.6 %all-to-all-start = ((f32[32,2,16,128]{3,2,1,0:T(8,128)}), f32[32,2,16,128]{3,2,1,0:T(8,128)S(1)}, u32[]{:S(2)}, u32[]{:S(2)}) async-start(f32[32,2,16,128]{3,2,1,0:T(8,128)} %get-tuple-element.29), calls=%async_computation | async-start | bytes 1048576 | tf_op jit(solution)/shard_map/all_to_all | solution.py:437

commit v5 on v4

--- a/solution.py
+++ b/solution.py
@@ -139,7 +139,7 @@
     return narrow(sublane_iota(LANES, lanes) < lax.broadcasted_iota(jnp.int32, (LANES, lanes), 1))
 
 
-def density_kernel(parts, bin_hbm, area_hbm, box_hbm, owner_hbm, dens_ref, top_ref, bottom_ref, starts_ref, s_ref, w_ref,
+def density_kernel(parts, bin_hbm, area_hbm, box_hbm, owner_hbm, dens_ref, top_ref, bottom_ref, starts_ref, s_ref, w_ref, code_ref,
                    a_ref, b_ref, bin_ref, area_ref, box_ref, owner_ref, pre_ref, cnt_ref, raw_ref, cong_ref, sem):
     pairs = ((bin_hbm, bin_ref), (area_hbm, area_ref), (box_hbm, box_ref), (owner_hbm, owner_ref))
     copies = [pltpu.make_async_copy(x, y, sem.at[k]) for k, (x, y) in enumerate(pairs)]
@@ -155,6 +155,7 @@
     s_ref[...] = ((bins >> 8) & 1) * TILE_R + (bins >> 9)
     w_ref[...] = (bins & 255) - LANES
     a_ref[...], b_ref[...] = halves(area)
+    code_ref[...] = area_code(area) * (TILE_R * TILE_C) + bins
     copies[2].wait()
     copies[3].wait()
     nil = jnp.zeros((), BF16)
@@ -235,7 +236,7 @@
     w_ref[...] = (dest & (LANES - 1)) + top * LANES - LANES
 
 
-def order_kernel(parts, starts_ref, s_ref, w_ref, bin_ref, area_ref, slots_ref, sorted_ref, a_ref, b_ref, c_ref, acc_ref, run_bin_ref, run_area_ref):
+def order_kernel(parts, starts_ref, s_ref, w_ref, code_ref, slots_ref, sorted_ref, a_ref, b_ref, c_ref, acc_ref, run_bin_ref, run_area_ref):
     all_rows = s_ref.shape[0]
     half = all_rows // 2
     group = all_rows // STEPS
@@ -243,8 +244,7 @@
 
     def encode(k):
         here = pl.ds(pl.multiple_of(k * group, group), group)
-        code = area_code(area_ref[here, :].astype(F32)) * (TILE_R * TILE_C) + bin_ref[here, :]
-        rest, last = divide(code, BASE)
+        rest, last = divide(code_ref[here, :], BASE)
         first, middle = divide(rest, BASE)
         a_ref[here, :] = symbol(first)
         b_ref[here, :] = symbol(middle)
@@ -402,12 +402,11 @@
     runs = vmem(rows + spare, LANES)
     table = shape(rows, LANES)
     grant = pltpu.CompilerParams(vmem_limit_bytes=GRANT)
-    whole_ints = shape(rows, LANES, dtype=jnp.int32)
     int_cells = vmem(rows, LANES, dtype=jnp.int32)
-    dens, top, bottom, starts, s, w = pl.pallas_call(
+    dens, top, bottom, starts, s, w, codes = pl.pallas_call(
         functools.partial(density_kernel, parts),
-        out_shape=(shape(TILE_R, TILE_C), shape(EDGE, TILE_C), shape(EDGE, TILE_C), shape(8, LANES, dtype=jnp.int32),
-                   whole_ints, whole_ints),
+        out_shape=(vmem(TILE_R, TILE_C), vmem(EDGE, TILE_C), vmem(EDGE, TILE_C), shape(8, LANES, dtype=jnp.int32),
+                   int_cells, int_cells, int_cells),
         in_specs=[pl.BlockSpec(memory_space=pltpu.HBM)] * 4,
         scratch_shapes=[cells, cells, int_cells, vmem(rows, LANES, dtype=BF16), vmem(*net_box.shape, dtype=jnp.int32), int_cells, cells, cells,
                         vmem(2 * LANES, 2 * LANES), vmem(TILE_C, 2 * TILE_R), pltpu.SemaphoreType.DMA((4,))],
@@ -421,13 +420,13 @@
     scalars = pl.BlockSpec(memory_space=pltpu.SMEM)
     slots, in_order = pl.pallas_call(
         functools.partial(order_kernel, parts),
-        out_shape=(shape(parts, 2, per, LANES), whole_ints),
-        in_specs=[scalars] + [pl.BlockSpec()] * 4,
+        out_shape=(vmem(parts, 2, per, LANES), int_cells),
+        in_specs=[scalars] + [pl.BlockSpec()] * 3,
         scratch_shapes=[cells, cells, cells, vmem(3 * LANES, 2 * LANES), runs, runs],
-        compiler_params=pltpu.CompilerParams(vmem_limit_bytes=FULL),
+        compiler_params=grant,
         cost_estimate=pl.CostEstimate(flops=15_000_000_000, bytes_accessed=2_000_000, transcendentals=0),
         name="order",
-    )(starts, s, w, bins, area)
+    )(starts, s, w, codes)
     up, down, slots = lax.optimization_barrier((up, down, slots))
     strip = jnp.concatenate([up, dens, down], axis=0)
     ahead = [(k, k + 1) for k in range(n_cols - 1)]
@@ -437,7 +436,7 @@
     first = lax.all_to_all(slots, ("rows", "cols"), 0, 0, tiled=True)
     density, shifts = pl.pallas_call(
         functools.partial(flow_kernel, parts, grid_rows, grid_cols),
-        out_shape=(shape(TILE_R, TILE_C), shape(parts, 2, per, LANES)),
+        out_shape=(shape(TILE_R, TILE_C), vmem(parts, 2, per, LANES)),
         in_specs=[scalars] + [pl.BlockSpec()] * 6,
         scratch_shapes=[vmem(TILE_R + 2 * EDGE, TILE_C + 2 * LANES), *[vmem(rows + spare, LANES)] * 4, vmem(2, 256, LANES)],
         compiler_params=grant,

time: 71.1 us -> 70.1 us (0.986)
  Pallas kernels: 29.3 us -> 28.5 us
    pallas_call x2, Pallas kernels: 16.5 us -> 15.6 us  [the longest x1 8.89 us: on_device(): pl.pallas_call(functools.partial(density_kernel, parts), out_shape=(vmem(...]
  transfers between devices with their start and end apart: 5 -> 5, of which waited for: 1 -> 1; matrix products, arithmetic and copies ran while one was open for 0% -> 0% of each run, Pallas kernels for 26% -> 25%
where the time goes in v5:
time: 70.1 us; the launch traced here: 69.8 us
  Pallas kernels  28.5 us (41%)
  blocking collectives  18.4 us (26%)
  starting transfers between devices  17.5 us (25%)
  waiting for transfers between devices  4.62 us (7%)
  between operations  0.74 us (1%)
    all_to_all x1, blocking collectives, on_device(): second = lax.all_to_all(shifts, ('rows', 'cols'), 0, 0, tiled=True)  18.4 us
    pallas_call x1, Pallas kernels, on_device(): pl.pallas_call(functools.partial(flow_kernel, parts, grid_rows, grid_cols...  11 us
    pallas_call x1, Pallas kernels, on_device(): pl.pallas_call(functools.partial(density_kernel, parts), out_shape=(vmem(...  8.89 us
    all_to_all x1, starting transfers between devices, on_device(): first = lax.all_to_all(slots, ('rows', 'cols'), 0, 0, tiled=True)  7.01 us
    pallas_call x1, Pallas kernels, on_device(): pl.pallas_call(functools.partial(order_kernel, parts), out_shape=(vmem(pa...  6.75 us
    ppermute x1, starting transfers between devices, on_device(): up = lax.ppermute(bottom, 'rows', ahead)  4.87 us
    all_to_all x1, waiting for transfers between devices, on_device(): first = lax.all_to_all(slots, ('rows', 'cols'), 0, 0, tiled=True)  4.61 us
    ppermute x1, starting transfers between devices, on_device(): left = lax.ppermute(strip[:, TILE_C - LANES:], 'cols', ahead)  3.03 us
  transfers between devices with their start and end apart: 5, of which 1 were waited for; matrix products, arithmetic and copies ran while one was open for 0% of the time, Pallas kernels for 25%

profile of v5, /device:TPU:0, one launch (start us, length us, event | category | flops | bytes accessed | tf_op | source)
XLA Modules:
  0.0 69.8 jit_solution(2323388781485632556)
XLA Ops:
  0.6 8.9 %density.1 = (f32[64,512]{1,0:T(8,128)S(1)}, f32[8,512]{1,0:T(8,128)S(1)}, f32[8,512]{1,0:T(8,128)S(1)}, s32[8,128]{1,0:T(8,128)}, s32[256,128]{1,0:T(8,128)S(1)...) custom-call(s32[256,128]{1,0:T(8,128)} %bitcast.4, bf16[256,128]{1,0:T(8,128)(2,1)} %bitcast.6, s32[4,16384]{1,0:T(4,128)} %box_hbm.1, ...), custom_call_target="tpu_custom_call" | custom-call | tf_op jit(solution)/shard_map/density/pallas_call | solution.py:406
  9.5 4.9 %collective-permute-start = (f32[8,512]{1,0:T(8,128)S(1)}, f32[8,512]{1,0:T(8,128)S(1)}, u32[]{:S(2)}, u32[]{:S(2)}) collective-permute-start(f32[8,512]{1,0:T(8,128)S(1)} %get-tuple-element.21), channel_id=1, source_target_pairs={{0,4},{4,8},{8,12},{12,16},{16,20},{20,24},{24,28},{1,5},{5,9},{9,... | collective-permute-start | bytes 49160 | tf_op jit(solution)/shard_map/ppermute | solution.py:418
  14.4 0.0 copy-start
  14.4 1.3 %collective-permute-start.1 = (f32[8,512]{1,0:T(8,128)S(1)}, f32[8,512]{1,0:T(8,128)S(1)}, u32[]{:S(2)}, u32[]{:S(2)}) collective-permute-start(f32[8,512]{1,0:T(8,128)S(1)} %get-tuple-element.22), channel_id=1, source_target_pairs={{4,0},{8,4},{12,8},{16,12},{20,16},{24,20},{28,24},{5,1},{9,5},{13... | collective-permute-start | bytes 49160 | tf_op jit(solution)/shard_map/ppermute | solution.py:419
  15.7 0.0 copy-done
  15.7 6.7 %order.1 = (f32[32,2,16,128]{3,2,1,0:T(8,128)}, s32[256,128]{1,0:T(8,128)S(1)}) custom-call(s32[8,128]{1,0:T(8,128)S(1)} %copy-done, s32[256,128]{1,0:T(8,128)S(1)} %get-tuple-element.23.s_ref, s32[256,128]{1,0:T(8,128)S(1)} %get-tuple-element.24.w_ref, s32[256,128]{1,0:T(8,128)S(1)} %get-tuple-element.25.code_ref), custom_call_target="tpu_custom_call" | custom-call | flops 15000000512 | bytes 2000000 | tf_op jit(solution)/shard_map/order/pallas_call | solution.py:421
  22.5 0.0 collective-permute-done.up_ref
  22.5 0.0 collective-permute-done.1.down_ref
  22.5 1.3 %collective-permute-start.3 = (f32[80,128]{1,0:T(8,128)S(1)}, f32[80,128]{1,0:T(8,128)S(1)}, u32[]{:S(2)}, u32[]{:S(2)}) collective-permute-start(f32[80,128]{1,0:T(8,128)S(1)} %get-tuple-element.35), channel_id=1, source_target_pairs={{1,0},{2,1},{3,2},{5,4},{6,5},{7,6},{9,8},{10,9},{11,10},{13,12},{... | collective-permute-start | bytes 122888 | tf_op jit(solution)/shard_map/ppermute | solution.py:435
  23.8 3.0 %collective-permute-start.2 = (f32[80,128]{1,0:T(8,128)S(1)}, f32[80,128]{1,0:T(8,128)S(1)}, u32[]{:S(2)}, u32[]{:S(2)}) collective-permute-start(f32[80,128]{1,0:T(8,128)S(1)} %get-tuple-element.36), channel_id=1, source_target_pairs={{0,1},{1,2},{2,3},{4,5},{5,6},{6,7},{8,9},{9,10},{10,11},{12,13},{... | collective-permute-start | bytes 122888 | tf_op jit(solution)/shard_map/ppermute | solution.py:434
  26.9 7.0 %all-to-all-start = ((f32[32,2,16,128]{3,2,1,0:T(8,128)}), f32[32,2,16,128]{3,2,1,0:T(8,128)S(1)}, u32[]{:S(2)}, u32[]{:S(2)}) async-start(f32[32,2,16,128]{3,2,1,0:T(8,128)} %get-tuple-element.31), calls=%async_computation | async-start | bytes 1048576 | tf_op jit(solution)/shard_map/all_to_all | solution.py:436
  33.9 0.0 collective-permute-done.3.right_ref
  33.9 0.0 collective-permute-done.2.left_ref
  33.9 11.0 %flow.1 = (f32[64,512]{1,0:T(8,128)}, f32[32,2,16,128]{3,2,1,0:T(8,128)S(1)}) custom-call(s32[8,128]{1,0:T(8,128)S(1)} %copy-done, f32[64,512]{1,0:T(8,128)S(1)} %get-tuple-element.20.dens_in, f32[8,512]{1,0:T(8,128)S(1)} %collective-permute-done.up_ref, f32[8,512]{1,0:T(8,128)S(1)} %collective-permute-done.1.down_ref, ...), custom_call_target="tpu_custom_call" | custom-call | flops 15000000512 | bytes 2000000 | tf_op jit(solution)/shard_map/flow/pallas_call | solution.py:437
  44.9 4.6 %all-to-all-done.first_ref = f32[32,2,16,128]{3,2,1,0:T(8,128)S(1)} async-done(((f32[32,2,16,128]{3,2,1,0:T(8,128)}), f32[32,2,16,128]{3,2,1,0:T(8,128)S(1)}, u32[]{:S(2)}, u32[]{:S(2)}) %all-to-all-start) | async-done | bytes 524320 | tf_op jit(solution)/shard_map/all_to_all | solution.py:436
  49.5 18.4 %all_to_all.10.second_ref = f32[32,2,16,128]{3,2,1,0:T(8,128)S(1)} all-to-all(f32[32,2,16,128]{3,2,1,0:T(8,128)S(1)} %get-tuple-element.32), channel_id=1, replica_groups=mesh['rows'=8,'cols'=4] {'rows','cols'}, dimensions={0} | all-to-all | bytes 1048576 | tf_op jit(solution)/shard_map/all_to_all | solution.py:446
  67.9 1.9 %merge.1 = (f32[3,65536]{1,0:T(4,128)}, s32[512,128]{1,0:T(8,128)}) custom-call(f32[32,2,16,128]{3,2,1,0:T(8,128)S(1)} %all-to-all-done.first_ref, f32[32,2,16,128]{3,2,1,0:T(8,128)S(1)} %all_to_all.10.second_ref), custom_call_target="tpu_custom_call" | custom-call | tf_op jit(solution)/shard_map/merge/pallas_call | solution.py:450
  (4 shorter events, 0.0 us)
Async XLA Ops:
  9.5 13.0 %collective-permute-start = (f32[8,512]{1,0:T(8,128)S(1)}, f32[8,512]{1,0:T(8,128)S(1)}, u32[]{:S(2)}, u32[]{:S(2)}) collective-permute-start(f32[8,512]{1,0:T(8,128)S(1)} %get-tuple-element.21), channel_id=1, source_target_pairs={{0,4},{4,8},{8,12},{12,16},{16,20},{20,24},{24,28},{1,5},{5,9},{9,... | collective-permute-start | bytes 49160 | tf_op jit(solution)/shard_map/ppermute | solution.py:418
  14.4 1.3 %copy-start = (s32[8,128]{1,0:T(8,128)S(1)}, s32[8,128]{1,0:T(8,128)}, u32[]{:S(2)}) copy-start(s32[8,128]{1,0:T(8,128)} %get-tuple-element.19.starts_ref) | copy-start | bytes 12292
  14.4 8.1 %collective-permute-start.1 = (f32[8,512]{1,0:T(8,128)S(1)}, f32[8,512]{1,0:T(8,128)S(1)}, u32[]{:S(2)}, u32[]{:S(2)}) collective-permute-start(f32[8,512]{1,0:T(8,128)S(1)} %get-tuple-element.22), channel_id=1, source_target_pairs={{4,0},{8,4},{12,8},{16,12},{20,16},{24,20},{28,24},{5,1},{9,5},{13... | collective-permute-start | bytes 49160 | tf_op jit(solution)/shard_map/ppermute | solution.py:419
  22.5 11.4 %collective-permute-start.3 = (f32[80,128]{1,0:T(8,128)S(1)}, f32[80,128]{1,0:T(8,128)S(1)}, u32[]{:S(2)}, u32[]{:S(2)}) collective-permute-start(f32[80,128]{1,0:T(8,128)S(1)} %get-tuple-element.35), channel_id=1, source_target_pairs={{1,0},{2,1},{3,2},{5,4},{6,5},{7,6},{9,8},{10,9},{11,10},{13,12},{... | collective-permute-start | bytes 122888 | tf_op jit(solution)/shard_map/ppermute | solution.py:435
  23.8 10.1 %collective-permute-start.2 = (f32[80,128]{1,0:T(8,128)S(1)}, f32[80,128]{1,0:T(8,128)S(1)}, u32[]{:S(2)}, u32[]{:S(2)}) collective-permute-start(f32[80,128]{1,0:T(8,128)S(1)} %get-tuple-element.36), channel_id=1, source_target_pairs={{0,1},{1,2},{2,3},{4,5},{5,6},{6,7},{8,9},{9,10},{10,11},{12,13},{... | collective-permute-start | bytes 122888 | tf_op jit(solution)/shard_map/ppermute | solution.py:434
  26.9 22.6 %all-to-all-start = ((f32[32,2,16,128]{3,2,1,0:T(8,128)}), f32[32,2,16,128]{3,2,1,0:T(8,128)S(1)}, u32[]{:S(2)}, u32[]{:S(2)}) async-start(f32[32,2,16,128]{3,2,1,0:T(8,128)} %get-tuple-element.31), calls=%async_computation | async-start | bytes 1048576 | tf_op jit(solution)/shard_map/all_to_all | solution.py:436

commit v6 on v5

--- a/solution.py
+++ b/solution.py
@@ -132,7 +132,7 @@
     return dot_nt(jnp.concatenate(left, axis=1), jnp.concatenate(right, axis=1))
 
 
-STEPS = 8
+STEPS = 4
 
 
 def before(lanes):
@@ -375,7 +375,7 @@
             out_ref[:, pl.ds(pl.multiple_of((k * per + r) * LANES, LANES), LANES)] = cells
         return carry
 
-    lax.fori_loop(0, parts, one_source, 0)
+    lax.fori_loop(0, parts, one_source, 0, unroll=4)
 
 
 def shape(*dims, dtype=F32):

time: 70.1 us -> 69 us (0.984)
  Pallas kernels: 28.5 us -> 27.4 us
where the time goes in v6:
time: 69 us; the launch traced here: 68.6 us
  Pallas kernels  27.4 us (40%)
  blocking collectives  18.4 us (27%)
  starting transfers between devices  17.5 us (25%)
  waiting for transfers between devices  4.62 us (7%)
  between operations  0.74 us (1%)
    all_to_all x1, blocking collectives, on_device(): second = lax.all_to_all(shifts, ('rows', 'cols'), 0, 0, tiled=True)  18.4 us
    pallas_call x1, Pallas kernels, on_device(): pl.pallas_call(functools.partial(flow_kernel, parts, grid_rows, grid_cols...  11 us
    pallas_call x1, Pallas kernels, on_device(): pl.pallas_call(functools.partial(density_kernel, parts), out_shape=(vmem(...  8.42 us
    all_to_all x1, starting transfers between devices, on_device(): first = lax.all_to_all(slots, ('rows', 'cols'), 0, 0, tiled=True)  7.01 us
    pallas_call x1, Pallas kernels, on_device(): pl.pallas_call(functools.partial(order_kernel, parts), out_shape=(vmem(pa...  6.2 us
    ppermute x1, starting transfers between devices, on_device(): up = lax.ppermute(bottom, 'rows', ahead)  4.87 us
    all_to_all x1, waiting for transfers between devices, on_device(): first = lax.all_to_all(slots, ('rows', 'cols'), 0, 0, tiled=True)  4.61 us
    ppermute x1, starting transfers between devices, on_device(): left = lax.ppermute(strip[:, TILE_C - LANES:], 'cols', ahead)  3.03 us
  transfers between devices with their start and end apart: 5, of which 1 were waited for; matrix products, arithmetic and copies ran while one was open for 0% of the time, Pallas kernels for 25%

profile of v6, /device:TPU:0, one launch (start us, length us, event | category | flops | bytes accessed | tf_op | source)
XLA Modules:
  0.0 68.6 jit_solution(8162013413884663279)
XLA Ops:
  0.6 8.4 %density.1 = (f32[64,512]{1,0:T(8,128)S(1)}, f32[8,512]{1,0:T(8,128)S(1)}, f32[8,512]{1,0:T(8,128)S(1)}, s32[8,128]{1,0:T(8,128)}, s32[256,128]{1,0:T(8,128)S(1)...) custom-call(s32[256,128]{1,0:T(8,128)} %bitcast.4, bf16[256,128]{1,0:T(8,128)(2,1)} %bitcast.6, s32[4,16384]{1,0:T(4,128)} %box_hbm.1, ...), custom_call_target="tpu_custom_call" | custom-call | tf_op jit(solution)/shard_map/density/pallas_call | solution.py:406
  9.1 4.9 %collective-permute-start = (f32[8,512]{1,0:T(8,128)S(1)}, f32[8,512]{1,0:T(8,128)S(1)}, u32[]{:S(2)}, u32[]{:S(2)}) collective-permute-start(f32[8,512]{1,0:T(8,128)S(1)} %get-tuple-element.21), channel_id=1, source_target_pairs={{0,4},{4,8},{8,12},{12,16},{16,20},{20,24},{24,28},{1,5},{5,9},{9,... | collective-permute-start | bytes 49160 | tf_op jit(solution)/shard_map/ppermute | solution.py:418
  13.9 0.0 copy-start
  13.9 1.3 %collective-permute-start.1 = (f32[8,512]{1,0:T(8,128)S(1)}, f32[8,512]{1,0:T(8,128)S(1)}, u32[]{:S(2)}, u32[]{:S(2)}) collective-permute-start(f32[8,512]{1,0:T(8,128)S(1)} %get-tuple-element.22), channel_id=1, source_target_pairs={{4,0},{8,4},{12,8},{16,12},{20,16},{24,20},{28,24},{5,1},{9,5},{13... | collective-permute-start | bytes 49160 | tf_op jit(solution)/shard_map/ppermute | solution.py:419
  15.2 0.0 copy-done
  15.3 6.2 %order.1 = (f32[32,2,16,128]{3,2,1,0:T(8,128)}, s32[256,128]{1,0:T(8,128)S(1)}) custom-call(s32[8,128]{1,0:T(8,128)S(1)} %copy-done, s32[256,128]{1,0:T(8,128)S(1)} %get-tuple-element.23.s_ref, s32[256,128]{1,0:T(8,128)S(1)} %get-tuple-element.24.w_ref, s32[256,128]{1,0:T(8,128)S(1)} %get-tuple-element.25.code_ref), custom_call_target="tpu_custom_call" | custom-call | flops 15000000512 | bytes 2000000 | tf_op jit(solution)/shard_map/order/pallas_call | solution.py:421
  21.5 0.0 collective-permute-done.up_ref
  21.5 0.0 collective-permute-done.1.down_ref
  21.5 1.3 %collective-permute-start.3 = (f32[80,128]{1,0:T(8,128)S(1)}, f32[80,128]{1,0:T(8,128)S(1)}, u32[]{:S(2)}, u32[]{:S(2)}) collective-permute-start(f32[80,128]{1,0:T(8,128)S(1)} %get-tuple-element.35), channel_id=1, source_target_pairs={{1,0},{2,1},{3,2},{5,4},{6,5},{7,6},{9,8},{10,9},{11,10},{13,12},{... | collective-permute-start | bytes 122888 | tf_op jit(solution)/shard_map/ppermute | solution.py:435
  22.8 3.0 %collective-permute-start.2 = (f32[80,128]{1,0:T(8,128)S(1)}, f32[80,128]{1,0:T(8,128)S(1)}, u32[]{:S(2)}, u32[]{:S(2)}) collective-permute-start(f32[80,128]{1,0:T(8,128)S(1)} %get-tuple-element.36), channel_id=1, source_target_pairs={{0,1},{1,2},{2,3},{4,5},{5,6},{6,7},{8,9},{9,10},{10,11},{12,13},{... | collective-permute-start | bytes 122888 | tf_op jit(solution)/shard_map/ppermute | solution.py:434
  25.9 7.0 %all-to-all-start = ((f32[32,2,16,128]{3,2,1,0:T(8,128)}), f32[32,2,16,128]{3,2,1,0:T(8,128)S(1)}, u32[]{:S(2)}, u32[]{:S(2)}) async-start(f32[32,2,16,128]{3,2,1,0:T(8,128)} %get-tuple-element.31), calls=%async_computation | async-start | bytes 1048576 | tf_op jit(solution)/shard_map/all_to_all | solution.py:436
  32.9 0.0 collective-permute-done.3.right_ref
  32.9 0.0 collective-permute-done.2.left_ref
  32.9 11.0 %flow.1 = (f32[64,512]{1,0:T(8,128)}, f32[32,2,16,128]{3,2,1,0:T(8,128)S(1)}) custom-call(s32[8,128]{1,0:T(8,128)S(1)} %copy-done, f32[64,512]{1,0:T(8,128)S(1)} %get-tuple-element.20.dens_in, f32[8,512]{1,0:T(8,128)S(1)} %collective-permute-done.up_ref, f32[8,512]{1,0:T(8,128)S(1)} %collective-permute-done.1.down_ref, ...), custom_call_target="tpu_custom_call" | custom-call | flops 15000000512 | bytes 2000000 | tf_op jit(solution)/shard_map/flow/pallas_call | solution.py:437
  43.9 4.6 %all-to-all-done.first_ref = f32[32,2,16,128]{3,2,1,0:T(8,128)S(1)} async-done(((f32[32,2,16,128]{3,2,1,0:T(8,128)}), f32[32,2,16,128]{3,2,1,0:T(8,128)S(1)}, u32[]{:S(2)}, u32[]{:S(2)}) %all-to-all-start) | async-done | bytes 524320 | tf_op jit(solution)/shard_map/all_to_all | solution.py:436
  48.5 18.4 %all_to_all.10.second_ref = f32[32,2,16,128]{3,2,1,0:T(8,128)S(1)} all-to-all(f32[32,2,16,128]{3,2,1,0:T(8,128)S(1)} %get-tuple-element.32), channel_id=1, replica_groups=mesh['rows'=8,'cols'=4] {'rows','cols'}, dimensions={0} | all-to-all | bytes 1048576 | tf_op jit(solution)/shard_map/all_to_all | solution.py:446
  66.9 1.8 %merge.1 = (f32[3,65536]{1,0:T(4,128)}, s32[512,128]{1,0:T(8,128)}) custom-call(f32[32,2,16,128]{3,2,1,0:T(8,128)S(1)} %all-to-all-done.first_ref, f32[32,2,16,128]{3,2,1,0:T(8,128)S(1)} %all_to_all.10.second_ref), custom_call_target="tpu_custom_call" | custom-call | tf_op jit(solution)/shard_map/merge/pallas_call | solution.py:450
  (4 shorter events, 0.0 us)
Async XLA Ops:
  9.1 12.4 %collective-permute-start = (f32[8,512]{1,0:T(8,128)S(1)}, f32[8,512]{1,0:T(8,128)S(1)}, u32[]{:S(2)}, u32[]{:S(2)}) collective-permute-start(f32[8,512]{1,0:T(8,128)S(1)} %get-tuple-element.21), channel_id=1, source_target_pairs={{0,4},{4,8},{8,12},{12,16},{16,20},{20,24},{24,28},{1,5},{5,9},{9,... | collective-permute-start | bytes 49160 | tf_op jit(solution)/shard_map/ppermute | solution.py:418
  13.9 1.3 %copy-start = (s32[8,128]{1,0:T(8,128)S(1)}, s32[8,128]{1,0:T(8,128)}, u32[]{:S(2)}) copy-start(s32[8,128]{1,0:T(8,128)} %get-tuple-element.19.starts_ref) | copy-start | bytes 12292
  13.9 7.5 %collective-permute-start.1 = (f32[8,512]{1,0:T(8,128)S(1)}, f32[8,512]{1,0:T(8,128)S(1)}, u32[]{:S(2)}, u32[]{:S(2)}) collective-permute-start(f32[8,512]{1,0:T(8,128)S(1)} %get-tuple-element.22), channel_id=1, source_target_pairs={{4,0},{8,4},{12,8},{16,12},{20,16},{24,20},{28,24},{5,1},{9,5},{13... | collective-permute-start | bytes 49160 | tf_op jit(solution)/shard_map/ppermute | solution.py:419
  21.5 11.4 %collective-permute-start.3 = (f32[80,128]{1,0:T(8,128)S(1)}, f32[80,128]{1,0:T(8,128)S(1)}, u32[]{:S(2)}, u32[]{:S(2)}) collective-permute-start(f32[80,128]{1,0:T(8,128)S(1)} %get-tuple-element.35), channel_id=1, source_target_pairs={{1,0},{2,1},{3,2},{5,4},{6,5},{7,6},{9,8},{10,9},{11,10},{13,12},{... | collective-permute-start | bytes 122888 | tf_op jit(solution)/shard_map/ppermute | solution.py:435
  22.8 10.1 %collective-permute-start.2 = (f32[80,128]{1,0:T(8,128)S(1)}, f32[80,128]{1,0:T(8,128)S(1)}, u32[]{:S(2)}, u32[]{:S(2)}) collective-permute-start(f32[80,128]{1,0:T(8,128)S(1)} %get-tuple-element.36), channel_id=1, source_target_pairs={{0,1},{1,2},{2,3},{4,5},{5,6},{6,7},{8,9},{9,10},{10,11},{12,13},{... | collective-permute-start | bytes 122888 | tf_op jit(solution)/shard_map/ppermute | solution.py:434
  25.9 22.6 %all-to-all-start = ((f32[32,2,16,128]{3,2,1,0:T(8,128)}), f32[32,2,16,128]{3,2,1,0:T(8,128)S(1)}, u32[]{:S(2)}, u32[]{:S(2)}) async-start(f32[32,2,16,128]{3,2,1,0:T(8,128)} %get-tuple-element.31), calls=%async_computation | async-start | bytes 1048576 | tf_op jit(solution)/shard_map/all_to_all | solution.py:436
